TPU v7x, 128 devices: a whole 4x4x4 slice. The times are simulated.
128 devices in a mesh: frame: 16 (over x, z), head: 8 (over y, core).
Axes of the slice: x: 4, y: 4, z: 4, core: 2. Of those that a mesh axis runs over, the one named last changes fastest.
Arguments:
- queries: bfloat16 [8192, 1024], P('frame', 'head'), may hold values from -6 to 6
- keys: bfloat16 [8192, 1024], P('frame', 'head'), may hold values from -6 to 6
- values: bfloat16 [8192, 1024], P('frame', 'head'), may hold values from -6 to 6
- band_width: int32 [16, 8], replicated, may hold values from 1 to 4, as said below
- band_offset: int32 [16, 8, 4], replicated, may hold values from 0 to 3
- out_weight: bfloat16 [1024, 1536], P('head'), may hold values from -0.1875 to 0.1875
Outputs:
- projected: bfloat16 [8192, 1536], P(('frame', 'head'))
Inputs may be any that keep to these rules, and one draw needn't show every extreme that they name: `band_width`: for distances 0 and 1 the widths lie in (2, 4], for 2 and 3 in (1, 2], for 4 to 7 in [1, 1]; each of these upper ends is reached by some frame.
All inputs are finite; a program needn't handle non-finite values.
Results may differ from a plain program's by a relative error of at most 0.015.
Values may be sent and summed in bfloat16 or wider, within the bound.
A program may use at most 64 MiB of HBM per device.

v0:
```python
import math

import jax
import jax.numpy as jnp
from jax import lax
from jax.sharding import PartitionSpec as P

HEAD = 128
BLK = 128
RADIUS = 7


def from_behind(value, axis, steps):
    count = lax.axis_size(axis)
    first, last = (max(0, -steps), min(count, count - steps))
    return lax.ppermute(value, axis, [(source, source + steps) for source in range(first, last)])


def block_mask(this_frame, key_frame, frames, band_width, band_offset, block_count):
    distance = jnp.abs(key_frame - this_frame)
    present = (key_frame >= 0) & (key_frame < frames) & (distance <= RADIUS)
    reach = jnp.minimum(distance, RADIUS)
    band_span = band_width[this_frame, reach]
    offsets = band_offset[this_frame, reach]
    query_block = lax.broadcasted_iota(jnp.int32, (block_count, block_count), 0)
    key_block = lax.broadcasted_iota(jnp.int32, (block_count, block_count), 1)
    inside = jnp.mod(key_block - offsets[:, None], block_count) < band_span
    diagonal = (reach == 0) & (query_block == key_block)
    return present & (inside | diagonal)


def absorb(running, query_heads, key_rows, value_rows, blocks):
    maxima, totals, weighted = running
    frame_tokens = query_heads.shape[0]
    local_heads = query_heads.shape[1]
    block_count = blocks.shape[0]
    score_scale = 1.0 / math.sqrt(HEAD)
    key_heads = key_rows.reshape(frame_tokens, local_heads, HEAD)
    value_heads = value_rows.reshape(frame_tokens, local_heads, HEAD)
    scores = (
        jnp.einsum("thd,shd->hts", query_heads, key_heads, preferred_element_type=jnp.float32)
        * score_scale
    )
    shaped = scores.reshape(local_heads, block_count, BLK, block_count, BLK)
    allowed = blocks[None, :, None, :, None]
    shaped = jnp.where(allowed, shaped, -1e30)
    block_peak = jnp.max(shaped, axis=(3, 4)).reshape(local_heads, frame_tokens)
    peak = jnp.maximum(maxima, block_peak)
    shifted = shaped - peak.reshape(local_heads, block_count, BLK, 1, 1)
    weights = jnp.where(allowed, jnp.exp(shifted), 0.0).reshape(
        local_heads, frame_tokens, frame_tokens
    )
    rescale = jnp.exp(maxima - peak)
    totals = totals * rescale + jnp.sum(weights, axis=2)
    update = jnp.einsum(
        "hts,shd->htd",
        weights.astype(jnp.bfloat16),
        value_heads,
        preferred_element_type=jnp.float32,
    )
    weighted = weighted * rescale[..., None] + update
    return (peak, totals, weighted)


def on_device(queries, keys, values, band_width, band_offset, out_weight):
    frame_tokens = queries.shape[0]
    local_heads = queries.shape[1] // HEAD
    block_count = frame_tokens // BLK
    frames = lax.axis_size("frame")
    this_frame = lax.axis_index("frame")
    query_heads = queries.reshape(frame_tokens, local_heads, HEAD)
    running = (
        jnp.full((local_heads, frame_tokens), -1e30, jnp.float32),
        jnp.zeros((local_heads, frame_tokens), jnp.float32),
        jnp.zeros((local_heads, frame_tokens, HEAD), jnp.float32),
    )

    def take(carry, key_rows, value_rows, key_frame):
        blocks = block_mask(this_frame, key_frame, frames, band_width, band_offset, block_count)
        return absorb(carry, query_heads, key_rows, value_rows, blocks)

    running = take(running, keys, values, this_frame)
    for step in range(1, RADIUS + 1):
        lower_keys, lower_values = from_behind((keys, values), "frame", step)
        running = take(running, lower_keys, lower_values, this_frame - step)
        upper_keys, upper_values = from_behind((keys, values), "frame", -step)
        running = take(running, upper_keys, upper_values, this_frame + step)
    maxima, totals, weighted = running
    attended = (weighted / totals[..., None]).transpose(1, 0, 2)
    attended = attended.reshape(frame_tokens, local_heads * HEAD).astype(jnp.bfloat16)
    token_rows = lax.all_to_all(attended, "head", split_axis=0, concat_axis=1, tiled=True)
    combined = jnp.dot(
        token_rows,
        lax.all_gather(out_weight, "head", axis=0, tiled=True),
        preferred_element_type=jnp.float32,
    )
    return combined.astype(jnp.bfloat16)


def solution(mesh):
    placed = (P("frame", "head"), P("frame", "head"), P("frame", "head"), P(), P(), P("head", None))
    return jax.shard_map(
        on_device, mesh=mesh, in_specs=placed, out_specs=P(("frame", "head"), None), check_vma=False
    )
```

profile of v0, /device:TPU:4, one launch (start us, length us, event | category | flops | bytes accessed | tf_op | source)
XLA Modules:
  0.0 171.9 jit_solution(5783069798436432417)
XLA Ops:
  6.5 5.8 %collective-permute-start.22 = (bf16[512,128]{1,0:T(8,128)(2,1)}, bf16[512,128]{1,0:T(8,128)(2,1)S(1)}, u32[]{:S(2)}, u32[]{:S(2)}) collective-permute-start(bf16[512,128]{1,0:T(8,128)(2,1)} %param.7), channel_id=1, source_target_pairs={{48,0},{56,8},{64,16},{72,24},{80,32},{88,40},{96,48},{104,56},{11... | collective-permute-start | bytes 393224 | tf_op jit(solution)/shard_map/ppermute | solution.py:16
  12.4 2.5 %collective-permute-start.20 = (bf16[512,128]{1,0:T(8,128)(2,1)}, bf16[512,128]{1,0:T(8,128)(2,1)S(1)}, u32[]{:S(2)}, u32[]{:S(2)}) collective-permute-start(bf16[512,128]{1,0:T(8,128)(2,1)} %param.7), channel_id=1, source_target_pairs={{0,48},{8,56},{16,64},{24,72},{32,80},{40,88},{48,96},{56,104},{64... | collective-permute-start | bytes 393224 | tf_op jit(solution)/shard_map/ppermute | solution.py:16
  14.9 7.4 %collective-permute-start.18 = (bf16[512,128]{1,0:T(8,128)(2,1)}, bf16[512,128]{1,0:T(8,128)(2,1)S(1)}, u32[]{:S(2)}, u32[]{:S(2)}) collective-permute-start(bf16[512,128]{1,0:T(8,128)(2,1)} %param.7), channel_id=1, source_target_pairs={{40,0},{48,8},{56,16},{64,24},{72,32},{80,40},{88,48},{96,56},{104... | collective-permute-start | bytes 393224 | tf_op jit(solution)/shard_map/ppermute | solution.py:16
  22.3 1.9 %collective-permute-start.16 = (bf16[512,128]{1,0:T(8,128)(2,1)}, bf16[512,128]{1,0:T(8,128)(2,1)S(1)}, u32[]{:S(2)}, u32[]{:S(2)}) collective-permute-start(bf16[512,128]{1,0:T(8,128)(2,1)} %param.7), channel_id=1, source_target_pairs={{0,40},{8,48},{16,56},{24,64},{32,72},{40,80},{48,88},{56,96},{64,... | collective-permute-start | bytes 393224 | tf_op jit(solution)/shard_map/ppermute | solution.py:16
  24.3 1.9 %collective-permute-start.14 = (bf16[512,128]{1,0:T(8,128)(2,1)}, bf16[512,128]{1,0:T(8,128)(2,1)S(1)}, u32[]{:S(2)}, u32[]{:S(2)}) collective-permute-start(bf16[512,128]{1,0:T(8,128)(2,1)} %param.7), channel_id=1, source_target_pairs={{32,0},{40,8},{48,16},{56,24},{64,32},{72,40},{80,48},{88,56},{96,... | collective-permute-start | bytes 393224 | tf_op jit(solution)/shard_map/ppermute | solution.py:16
  26.3 1.7 constant_dynamic-slice_fusion.7
  27.9 1.1 fusion.140
  29.1 1.3 broadcast_and_fusion.1
  30.7 1.3 fusion.192
  31.9 1.2 broadcast_and_fusion.3
  33.2 1.3 broadcast_and_fusion.7
  34.5 1.1 broadcast_and_fusion.11
  35.6 3.9 %collective-permute-start.12 = (bf16[512,128]{1,0:T(8,128)(2,1)}, bf16[512,128]{1,0:T(8,128)(2,1)S(1)}, u32[]{:S(2)}, u32[]{:S(2)}) collective-permute-start(bf16[512,128]{1,0:T(8,128)(2,1)} %param.7), channel_id=1, source_target_pairs={{0,32},{8,40},{16,48},{24,56},{32,64},{40,72},{48,80},{56,88},{64,... | collective-permute-start | bytes 393224 | tf_op jit(solution)/shard_map/ppermute | solution.py:16
  39.8 0.4 fusion.180
  40.2 1.9 %collective-permute-start.10 = (bf16[512,128]{1,0:T(8,128)(2,1)S(1)}, bf16[512,128]{1,0:T(8,128)(2,1)S(1)}, u32[]{:S(2)}, u32[]{:S(2)}) collective-permute-start(bf16[512,128]{1,0:T(8,128)(2,1)S(1)} %copy-done.1), channel_id=1, source_target_pairs={{24,0},{32,8},{40,16},{48,24},{56,32},{64,40},{72,48},{80,56},{88,... | collective-permute-start | bytes 393224 | tf_op jit(solution)/shard_map/ppermute | solution.py:16
  42.3 0.4 fusion.181
  42.7 6.1 %collective-permute-start.8 = (bf16[512,128]{1,0:T(8,128)(2,1)S(1)}, bf16[512,128]{1,0:T(8,128)(2,1)S(1)}, u32[]{:S(2)}, u32[]{:S(2)}) collective-permute-start(bf16[512,128]{1,0:T(8,128)(2,1)S(1)} %copy-done.1), channel_id=1, source_target_pairs={{0,24},{8,32},{16,40},{24,48},{32,56},{40,64},{48,72},{56,80},{64,... | collective-permute-start | bytes 393224 | tf_op jit(solution)/shard_map/ppermute | solution.py:16
  49.0 0.4 fusion.182
  49.4 4.8 %collective-permute-start.6 = (bf16[512,128]{1,0:T(8,128)(2,1)S(1)}, bf16[512,128]{1,0:T(8,128)(2,1)S(1)}, u32[]{:S(2)}, u32[]{:S(2)}) collective-permute-start(bf16[512,128]{1,0:T(8,128)(2,1)S(1)} %copy-done.1), channel_id=1, source_target_pairs={{16,0},{24,8},{32,16},{40,24},{48,32},{56,40},{64,48},{72,56},{80,... | collective-permute-start | bytes 393224 | tf_op jit(solution)/shard_map/ppermute | solution.py:16
  54.4 0.4 fusion.183
  54.8 2.5 %collective-permute-start.4 = (bf16[512,128]{1,0:T(8,128)(2,1)S(1)}, bf16[512,128]{1,0:T(8,128)(2,1)S(1)}, u32[]{:S(2)}, u32[]{:S(2)}) collective-permute-start(bf16[512,128]{1,0:T(8,128)(2,1)S(1)} %copy-done.1), channel_id=1, source_target_pairs={{0,16},{8,24},{16,32},{24,40},{32,48},{40,56},{48,64},{56,72},{64,... | collective-permute-start | bytes 393224 | tf_op jit(solution)/shard_map/ppermute | solution.py:16
  57.5 0.4 fusion.184
  57.9 7.2 %collective-permute-start.2 = (bf16[512,128]{1,0:T(8,128)(2,1)S(1)}, bf16[512,128]{1,0:T(8,128)(2,1)S(1)}, u32[]{:S(2)}, u32[]{:S(2)}) collective-permute-start(bf16[512,128]{1,0:T(8,128)(2,1)S(1)} %copy-done.1), channel_id=1, source_target_pairs={{8,0},{16,8},{24,16},{32,24},{40,32},{48,40},{56,48},{64,56},{72,6... | collective-permute-start | bytes 393224 | tf_op jit(solution)/shard_map/ppermute | solution.py:16
  65.7 1.9 %collective-permute-start = (bf16[512,128]{1,0:T(8,128)(2,1)S(1)}, bf16[512,128]{1,0:T(8,128)(2,1)S(1)}, u32[]{:S(2)}, u32[]{:S(2)}) collective-permute-start(bf16[512,128]{1,0:T(8,128)(2,1)S(1)} %copy-done.1), channel_id=1, source_target_pairs={{0,8},{8,16},{16,24},{24,32},{32,40},{40,48},{48,56},{56,64},{64,7... | collective-permute-start | bytes 393224 | tf_op jit(solution)/shard_map/ppermute | solution.py:16
  68.2 1.9 %collective-permute-start.26 = (bf16[512,128]{1,0:T(8,128)(2,1)S(1)}, bf16[512,128]{1,0:T(8,128)(2,1)S(1)}, u32[]{:S(2)}, u32[]{:S(2)}) collective-permute-start(bf16[512,128]{1,0:T(8,128)(2,1)S(1)} %copy-done.1), channel_id=1, source_target_pairs={{56,0},{64,8},{72,16},{80,24},{88,32},{96,40},{104,48},{112,56},{1... | collective-permute-start | bytes 393224 | tf_op jit(solution)/shard_map/ppermute | solution.py:16
  70.3 0.4 fusion.187
  70.7 6.0 %collective-permute-start.24 = (bf16[512,128]{1,0:T(8,128)(2,1)S(1)}, bf16[512,128]{1,0:T(8,128)(2,1)S(1)}, u32[]{:S(2)}, u32[]{:S(2)}) collective-permute-start(bf16[512,128]{1,0:T(8,128)(2,1)S(1)} %copy-done.1), channel_id=1, source_target_pairs={{0,56},{8,64},{16,72},{24,80},{32,88},{40,96},{48,104},{56,112},{6... | collective-permute-start | bytes 393224 | tf_op jit(solution)/shard_map/ppermute | solution.py:16
  76.9 0.4 fusion.188
  77.3 1.9 %collective-permute-start.17 = (bf16[512,128]{1,0:T(8,128)(2,1)S(1)}, bf16[512,128]{1,0:T(8,128)(2,1)S(1)}, u32[]{:S(2)}, u32[]{:S(2)}) collective-permute-start(bf16[512,128]{1,0:T(8,128)(2,1)S(1)} %copy-done.2), channel_id=1, source_target_pairs={{0,40},{8,48},{16,56},{24,64},{32,72},{40,80},{48,88},{56,96},{64,... | collective-permute-start | bytes 393224 | tf_op jit(solution)/shard_map/ppermute | solution.py:16
  79.5 0.4 fusion.189
  79.8 1.9 %collective-permute-start.15 = (bf16[512,128]{1,0:T(8,128)(2,1)S(1)}, bf16[512,128]{1,0:T(8,128)(2,1)S(1)}, u32[]{:S(2)}, u32[]{:S(2)}) collective-permute-start(bf16[512,128]{1,0:T(8,128)(2,1)S(1)} %copy-done.2), channel_id=1, source_target_pairs={{32,0},{40,8},{48,16},{56,24},{64,32},{72,40},{80,48},{88,56},{96,... | collective-permute-start | bytes 393224 | tf_op jit(solution)/shard_map/ppermute | solution.py:16
  82.0 0.4 fusion.190
  82.3 3.9 %collective-permute-start.13 = (bf16[512,128]{1,0:T(8,128)(2,1)S(1)}, bf16[512,128]{1,0:T(8,128)(2,1)S(1)}, u32[]{:S(2)}, u32[]{:S(2)}) collective-permute-start(bf16[512,128]{1,0:T(8,128)(2,1)S(1)} %copy-done.2), channel_id=1, source_target_pairs={{0,32},{8,40},{16,48},{24,56},{32,64},{40,72},{48,80},{56,88},{64,... | collective-permute-start | bytes 393224 | tf_op jit(solution)/shard_map/ppermute | solution.py:16
  86.8 3.6 %collective-permute-start.11 = (bf16[512,128]{1,0:T(8,128)(2,1)S(1)}, bf16[512,128]{1,0:T(8,128)(2,1)S(1)}, u32[]{:S(2)}, u32[]{:S(2)}) collective-permute-start(bf16[512,128]{1,0:T(8,128)(2,1)S(1)} %copy-done.2), channel_id=1, source_target_pairs={{24,0},{32,8},{40,16},{48,24},{56,32},{64,40},{72,48},{80,56},{88,... | collective-permute-start | bytes 393224 | tf_op jit(solution)/shard_map/ppermute | solution.py:16
  90.7 0.4 fusion.178
  91.1 3.6 %collective-permute-start.9 = (bf16[512,128]{1,0:T(8,128)(2,1)S(1)}, bf16[512,128]{1,0:T(8,128)(2,1)S(1)}, u32[]{:S(2)}, u32[]{:S(2)}) collective-permute-start(bf16[512,128]{1,0:T(8,128)(2,1)S(1)} %copy-done.2), channel_id=1, source_target_pairs={{0,24},{8,32},{16,40},{24,48},{32,56},{40,64},{48,72},{56,80},{64,... | collective-permute-start | bytes 393224 | tf_op jit(solution)/shard_map/ppermute | solution.py:16
  94.9 0.4 fusion.179
  99.7 0.5 fusion.15
  100.2 6.9 %collective-permute-start.7 = (bf16[512,128]{1,0:T(8,128)(2,1)S(1)}, bf16[512,128]{1,0:T(8,128)(2,1)S(1)}, u32[]{:S(2)}, u32[]{:S(2)}) collective-permute-start(bf16[512,128]{1,0:T(8,128)(2,1)S(1)} %copy-done.2), channel_id=1, source_target_pairs={{16,0},{24,8},{32,16},{40,24},{48,32},{56,40},{64,48},{72,56},{80,... | collective-permute-start | bytes 393224 | tf_op jit(solution)/shard_map/ppermute | solution.py:16
  107.1 0.5 fusion.84
  107.6 1.9 %collective-permute-start.5 = (bf16[512,128]{1,0:T(8,128)(2,1)S(1)}, bf16[512,128]{1,0:T(8,128)(2,1)S(1)}, u32[]{:S(2)}, u32[]{:S(2)}) collective-permute-start(bf16[512,128]{1,0:T(8,128)(2,1)S(1)} %copy-done.2), channel_id=1, source_target_pairs={{0,16},{8,24},{16,32},{24,40},{32,48},{40,56},{48,64},{56,72},{64,... | collective-permute-start | bytes 393224 | tf_op jit(solution)/shard_map/ppermute | solution.py:16
  109.5 0.4 fusion.86
  110.0 5.4 %collective-permute-start.3 = (bf16[512,128]{1,0:T(8,128)(2,1)S(1)}, bf16[512,128]{1,0:T(8,128)(2,1)S(1)}, u32[]{:S(2)}, u32[]{:S(2)}) collective-permute-start(bf16[512,128]{1,0:T(8,128)(2,1)S(1)} %copy-done.2), channel_id=1, source_target_pairs={{8,0},{16,8},{24,16},{32,24},{40,32},{48,40},{56,48},{64,56},{72,6... | collective-permute-start | bytes 393224 | tf_op jit(solution)/shard_map/ppermute | solution.py:16
  115.4 0.4 fusion.88
  115.9 4.8 %collective-permute-start.19 = (bf16[512,128]{1,0:T(8,128)(2,1)S(1)}, bf16[512,128]{1,0:T(8,128)(2,1)S(1)}, u32[]{:S(2)}, u32[]{:S(2)}) collective-permute-start(bf16[512,128]{1,0:T(8,128)(2,1)S(1)} %copy-done.2), channel_id=1, source_target_pairs={{40,0},{48,8},{56,16},{64,24},{72,32},{80,40},{88,48},{96,56},{104... | collective-permute-start | bytes 393224 | tf_op jit(solution)/shard_map/ppermute | solution.py:16
  120.7 0.4 fusion.90
  121.1 1.9 %collective-permute-start.21 = (bf16[512,128]{1,0:T(8,128)(2,1)S(1)}, bf16[512,128]{1,0:T(8,128)(2,1)S(1)}, u32[]{:S(2)}, u32[]{:S(2)}) collective-permute-start(bf16[512,128]{1,0:T(8,128)(2,1)S(1)} %copy-done.2), channel_id=1, source_target_pairs={{0,48},{8,56},{16,64},{24,72},{32,80},{40,88},{48,96},{56,104},{64... | collective-permute-start | bytes 393224 | tf_op jit(solution)/shard_map/ppermute | solution.py:16
  123.1 0.4 fusion.92
  123.5 7.8 %collective-permute-start.23 = (bf16[512,128]{1,0:T(8,128)(2,1)S(1)}, bf16[512,128]{1,0:T(8,128)(2,1)S(1)}, u32[]{:S(2)}, u32[]{:S(2)}) collective-permute-start(bf16[512,128]{1,0:T(8,128)(2,1)S(1)} %copy-done.2), channel_id=1, source_target_pairs={{48,0},{56,8},{64,16},{72,24},{80,32},{88,40},{96,48},{104,56},{11... | collective-permute-start | bytes 393224 | tf_op jit(solution)/shard_map/ppermute | solution.py:16
  131.4 0.4 fusion.94
  131.8 1.9 %collective-permute-start.25 = (bf16[512,128]{1,0:T(8,128)(2,1)S(1)}, bf16[512,128]{1,0:T(8,128)(2,1)S(1)}, u32[]{:S(2)}, u32[]{:S(2)}) collective-permute-start(bf16[512,128]{1,0:T(8,128)(2,1)S(1)} %copy-done.2), channel_id=1, source_target_pairs={{0,56},{8,64},{16,72},{24,80},{32,88},{40,96},{48,104},{56,112},{6... | collective-permute-start | bytes 393224 | tf_op jit(solution)/shard_map/ppermute | solution.py:16
  133.7 0.4 fusion.96
  134.2 6.3 %collective-permute-start.27 = (bf16[512,128]{1,0:T(8,128)(2,1)S(1)}, bf16[512,128]{1,0:T(8,128)(2,1)S(1)}, u32[]{:S(2)}, u32[]{:S(2)}) collective-permute-start(bf16[512,128]{1,0:T(8,128)(2,1)S(1)} %copy-done.2), channel_id=1, source_target_pairs={{56,0},{64,8},{72,16},{80,24},{88,32},{96,40},{104,48},{112,56},{1... | collective-permute-start | bytes 393224 | tf_op jit(solution)/shard_map/ppermute | solution.py:16
  140.5 0.4 fusion.98
  141.0 2.2 %collective-permute-start.1 = (bf16[512,128]{1,0:T(8,128)(2,1)S(1)}, bf16[512,128]{1,0:T(8,128)(2,1)S(1)}, u32[]{:S(2)}, u32[]{:S(2)}) collective-permute-start(bf16[512,128]{1,0:T(8,128)(2,1)S(1)} %copy-done.2), channel_id=1, source_target_pairs={{0,8},{8,16},{16,24},{24,32},{32,40},{40,48},{48,56},{56,64},{64,7... | collective-permute-start | bytes 393224 | tf_op jit(solution)/shard_map/ppermute | solution.py:16
  143.2 0.5 fusion.82
  143.7 0.5 fusion.80
  144.1 0.5 fusion.78
  144.6 0.4 fusion.76
  145.1 0.5 fusion.74
  145.5 4.4 %collective-permute-done.1 = bf16[512,128]{1,0:T(8,128)(2,1)S(1)} collective-permute-done((bf16[512,128]{1,0:T(8,128)(2,1)S(1)}, bf16[512,128]{1,0:T(8,128)(2,1)S(1)}, u32[]{:S(2)}, u32[]{:S(2)}) %collective-permute-start.1) | collective-permute-done | bytes 131104 | tf_op jit(solution)/shard_map/ppermute | solution.py:16
  149.9 1.5 fusion.43
  151.4 10.4 %all_to_all.16 = bf16[8,64,128]{2,1,0:T(8,128)(2,1)S(1)} all-to-all(bf16[8,64,128]{2,1,0:T(8,128)(2,1)S(1)} %bitcast.288), channel_id=1, replica_groups=mesh['frame'=16,'head'=8] {'head'}, dimensions={0} | all-to-all | bytes 262144 | tf_op jit(solution)/shard_map/all_to_all | solution.py:91
  161.8 3.2 %convolution_convert_fusion = bf16[64,1536]{1,0:T(8,128)(2,1)} fusion(bf16[1024,1536]{1,0:T(8,128)(2,1)} %all-gather.2.cloned.1.call-done, bf16[8,64,128]{2,1,0:T(8,128)(2,1)S(1)} %all_to_all.16), kind=kOutput, calls=%fused_computation | convolution fusion | flops 201424896 | bytes 3473408 | tf_op jit(solution)/shard_map/dot_general | solution.py:92
  (71 shorter events, 8.7 us)
Async XLA Ops:
  6.5 24.1 %copy-start = (bf16[512,128]{1,0:T(8,128)(2,1)S(1)}, bf16[512,128]{1,0:T(8,128)(2,1)}, u32[]{:S(2)}) copy-start(bf16[512,128]{1,0:T(8,128)(2,1)} %param.6) | copy-start | bytes 393220
  6.5 33.6 %copy-start.1 = (bf16[512,128]{1,0:T(8,128)(2,1)S(1)}, bf16[512,128]{1,0:T(8,128)(2,1)}, u32[]{:S(2)}) copy-start(bf16[512,128]{1,0:T(8,128)(2,1)} %param.7) | copy-start | bytes 393220
  6.5 155.3 %all-gather.2.cloned.1.call-start = ((), (), s32[]{:S(2)}) async-start(), calls=%async_computation.1 | async-start | bytes 3538944 | tf_op jit(solution)/shard_map/all_gather | solution.py:94
  6.5 29.1 %collective-permute-start.22 = (bf16[512,128]{1,0:T(8,128)(2,1)}, bf16[512,128]{1,0:T(8,128)(2,1)S(1)}, u32[]{:S(2)}, u32[]{:S(2)}) collective-permute-start(bf16[512,128]{1,0:T(8,128)(2,1)} %param.7), channel_id=1, source_target_pairs={{48,0},{56,8},{64,16},{72,24},{80,32},{88,40},{96,48},{104,56},{11... | collective-permute-start | bytes 393224 | tf_op jit(solution)/shard_map/ppermute | solution.py:16
  12.4 27.7 %collective-permute-start.20 = (bf16[512,128]{1,0:T(8,128)(2,1)}, bf16[512,128]{1,0:T(8,128)(2,1)S(1)}, u32[]{:S(2)}, u32[]{:S(2)}) collective-permute-start(bf16[512,128]{1,0:T(8,128)(2,1)} %param.7), channel_id=1, source_target_pairs={{0,48},{8,56},{16,64},{24,72},{32,80},{40,88},{48,96},{56,104},{64... | collective-permute-start | bytes 393224 | tf_op jit(solution)/shard_map/ppermute | solution.py:16
  14.9 27.7 %collective-permute-start.18 = (bf16[512,128]{1,0:T(8,128)(2,1)}, bf16[512,128]{1,0:T(8,128)(2,1)S(1)}, u32[]{:S(2)}, u32[]{:S(2)}) collective-permute-start(bf16[512,128]{1,0:T(8,128)(2,1)} %param.7), channel_id=1, source_target_pairs={{40,0},{48,8},{56,16},{64,24},{72,32},{80,40},{88,48},{96,56},{104... | collective-permute-start | bytes 393224 | tf_op jit(solution)/shard_map/ppermute | solution.py:16
  22.3 27.0 %collective-permute-start.16 = (bf16[512,128]{1,0:T(8,128)(2,1)}, bf16[512,128]{1,0:T(8,128)(2,1)S(1)}, u32[]{:S(2)}, u32[]{:S(2)}) collective-permute-start(bf16[512,128]{1,0:T(8,128)(2,1)} %param.7), channel_id=1, source_target_pairs={{0,40},{8,48},{16,56},{24,64},{32,72},{40,80},{48,88},{56,96},{64,... | collective-permute-start | bytes 393224 | tf_op jit(solution)/shard_map/ppermute | solution.py:16
  24.3 30.5 %collective-permute-start.14 = (bf16[512,128]{1,0:T(8,128)(2,1)}, bf16[512,128]{1,0:T(8,128)(2,1)S(1)}, u32[]{:S(2)}, u32[]{:S(2)}) collective-permute-start(bf16[512,128]{1,0:T(8,128)(2,1)} %param.7), channel_id=1, source_target_pairs={{32,0},{40,8},{48,16},{56,24},{64,32},{72,40},{80,48},{88,56},{96,... | collective-permute-start | bytes 393224 | tf_op jit(solution)/shard_map/ppermute | solution.py:16
  35.6 22.3 %collective-permute-start.12 = (bf16[512,128]{1,0:T(8,128)(2,1)}, bf16[512,128]{1,0:T(8,128)(2,1)S(1)}, u32[]{:S(2)}, u32[]{:S(2)}) collective-permute-start(bf16[512,128]{1,0:T(8,128)(2,1)} %param.7), channel_id=1, source_target_pairs={{0,32},{8,40},{16,48},{24,56},{32,64},{40,72},{48,80},{56,88},{64,... | collective-permute-start | bytes 393224 | tf_op jit(solution)/shard_map/ppermute | solution.py:16
  40.2 25.5 %collective-permute-start.10 = (bf16[512,128]{1,0:T(8,128)(2,1)S(1)}, bf16[512,128]{1,0:T(8,128)(2,1)S(1)}, u32[]{:S(2)}, u32[]{:S(2)}) collective-permute-start(bf16[512,128]{1,0:T(8,128)(2,1)S(1)} %copy-done.1), channel_id=1, source_target_pairs={{24,0},{32,8},{40,16},{48,24},{56,32},{64,40},{72,48},{80,56},{88,... | collective-permute-start | bytes 393224 | tf_op jit(solution)/shard_map/ppermute | solution.py:16
  42.7 25.5 %collective-permute-start.8 = (bf16[512,128]{1,0:T(8,128)(2,1)S(1)}, bf16[512,128]{1,0:T(8,128)(2,1)S(1)}, u32[]{:S(2)}, u32[]{:S(2)}) collective-permute-start(bf16[512,128]{1,0:T(8,128)(2,1)S(1)} %copy-done.1), channel_id=1, source_target_pairs={{0,24},{8,32},{16,40},{24,48},{32,56},{40,64},{48,72},{56,80},{64,... | collective-permute-start | bytes 393224 | tf_op jit(solution)/shard_map/ppermute | solution.py:16
  49.4 21.3 %collective-permute-start.6 = (bf16[512,128]{1,0:T(8,128)(2,1)S(1)}, bf16[512,128]{1,0:T(8,128)(2,1)S(1)}, u32[]{:S(2)}, u32[]{:S(2)}) collective-permute-start(bf16[512,128]{1,0:T(8,128)(2,1)S(1)} %copy-done.1), channel_id=1, source_target_pairs={{16,0},{24,8},{32,16},{40,24},{48,32},{56,40},{64,48},{72,56},{80,... | collective-permute-start | bytes 393224 | tf_op jit(solution)/shard_map/ppermute | solution.py:16
  54.8 22.5 %collective-permute-start.4 = (bf16[512,128]{1,0:T(8,128)(2,1)S(1)}, bf16[512,128]{1,0:T(8,128)(2,1)S(1)}, u32[]{:S(2)}, u32[]{:S(2)}) collective-permute-start(bf16[512,128]{1,0:T(8,128)(2,1)S(1)} %copy-done.1), channel_id=1, source_target_pairs={{0,16},{8,24},{16,32},{24,40},{32,48},{40,56},{48,64},{56,72},{64,... | collective-permute-start | bytes 393224 | tf_op jit(solution)/shard_map/ppermute | solution.py:16
  57.9 21.9 %collective-permute-start.2 = (bf16[512,128]{1,0:T(8,128)(2,1)S(1)}, bf16[512,128]{1,0:T(8,128)(2,1)S(1)}, u32[]{:S(2)}, u32[]{:S(2)}) collective-permute-start(bf16[512,128]{1,0:T(8,128)(2,1)S(1)} %copy-done.1), channel_id=1, source_target_pairs={{8,0},{16,8},{24,16},{32,24},{40,32},{48,40},{56,48},{64,56},{72,6... | collective-permute-start | bytes 393224 | tf_op jit(solution)/shard_map/ppermute | solution.py:16
  65.7 16.7 %collective-permute-start = (bf16[512,128]{1,0:T(8,128)(2,1)S(1)}, bf16[512,128]{1,0:T(8,128)(2,1)S(1)}, u32[]{:S(2)}, u32[]{:S(2)}) collective-permute-start(bf16[512,128]{1,0:T(8,128)(2,1)S(1)} %copy-done.1), channel_id=1, source_target_pairs={{0,8},{8,16},{16,24},{24,32},{32,40},{40,48},{48,56},{56,64},{64,7... | collective-permute-start | bytes 393224 | tf_op jit(solution)/shard_map/ppermute | solution.py:16
  67.8 9.5 %copy-start.2 = (bf16[512,128]{1,0:T(8,128)(2,1)S(1)}, bf16[512,128]{1,0:T(8,128)(2,1)}, u32[]{:S(2)}) copy-start(bf16[512,128]{1,0:T(8,128)(2,1)} %param.8) | copy-start | bytes 393220
  68.2 18.7 %collective-permute-start.26 = (bf16[512,128]{1,0:T(8,128)(2,1)S(1)}, bf16[512,128]{1,0:T(8,128)(2,1)S(1)}, u32[]{:S(2)}, u32[]{:S(2)}) collective-permute-start(bf16[512,128]{1,0:T(8,128)(2,1)S(1)} %copy-done.1), channel_id=1, source_target_pairs={{56,0},{64,8},{72,16},{80,24},{88,32},{96,40},{104,48},{112,56},{1... | collective-permute-start | bytes 393224 | tf_op jit(solution)/shard_map/ppermute | solution.py:16
  70.7 20.4 %collective-permute-start.24 = (bf16[512,128]{1,0:T(8,128)(2,1)S(1)}, bf16[512,128]{1,0:T(8,128)(2,1)S(1)}, u32[]{:S(2)}, u32[]{:S(2)}) collective-permute-start(bf16[512,128]{1,0:T(8,128)(2,1)S(1)} %copy-done.1), channel_id=1, source_target_pairs={{0,56},{8,64},{16,72},{24,80},{32,88},{40,96},{48,104},{56,112},{6... | collective-permute-start | bytes 393224 | tf_op jit(solution)/shard_map/ppermute | solution.py:16
  77.3 22.9 %collective-permute-start.17 = (bf16[512,128]{1,0:T(8,128)(2,1)S(1)}, bf16[512,128]{1,0:T(8,128)(2,1)S(1)}, u32[]{:S(2)}, u32[]{:S(2)}) collective-permute-start(bf16[512,128]{1,0:T(8,128)(2,1)S(1)} %copy-done.2), channel_id=1, source_target_pairs={{0,40},{8,48},{16,56},{24,64},{32,72},{40,80},{48,88},{56,96},{64,... | collective-permute-start | bytes 393224 | tf_op jit(solution)/shard_map/ppermute | solution.py:16
  79.8 27.8 %collective-permute-start.15 = (bf16[512,128]{1,0:T(8,128)(2,1)S(1)}, bf16[512,128]{1,0:T(8,128)(2,1)S(1)}, u32[]{:S(2)}, u32[]{:S(2)}) collective-permute-start(bf16[512,128]{1,0:T(8,128)(2,1)S(1)} %copy-done.2), channel_id=1, source_target_pairs={{32,0},{40,8},{48,16},{56,24},{64,32},{72,40},{80,48},{88,56},{96,... | collective-permute-start | bytes 393224 | tf_op jit(solution)/shard_map/ppermute | solution.py:16
  82.3 27.6 %collective-permute-start.13 = (bf16[512,128]{1,0:T(8,128)(2,1)S(1)}, bf16[512,128]{1,0:T(8,128)(2,1)S(1)}, u32[]{:S(2)}, u32[]{:S(2)}) collective-permute-start(bf16[512,128]{1,0:T(8,128)(2,1)S(1)} %copy-done.2), channel_id=1, source_target_pairs={{0,32},{8,40},{16,48},{24,56},{32,64},{40,72},{48,80},{56,88},{64,... | collective-permute-start | bytes 393224 | tf_op jit(solution)/shard_map/ppermute | solution.py:16
  86.8 29.0 %collective-permute-start.11 = (bf16[512,128]{1,0:T(8,128)(2,1)S(1)}, bf16[512,128]{1,0:T(8,128)(2,1)S(1)}, u32[]{:S(2)}, u32[]{:S(2)}) collective-permute-start(bf16[512,128]{1,0:T(8,128)(2,1)S(1)} %copy-done.2), channel_id=1, source_target_pairs={{24,0},{32,8},{40,16},{48,24},{56,32},{64,40},{72,48},{80,56},{88,... | collective-permute-start | bytes 393224 | tf_op jit(solution)/shard_map/ppermute | solution.py:16
  91.1 30.1 %collective-permute-start.9 = (bf16[512,128]{1,0:T(8,128)(2,1)S(1)}, bf16[512,128]{1,0:T(8,128)(2,1)S(1)}, u32[]{:S(2)}, u32[]{:S(2)}) collective-permute-start(bf16[512,128]{1,0:T(8,128)(2,1)S(1)} %copy-done.2), channel_id=1, source_target_pairs={{0,24},{8,32},{16,40},{24,48},{32,56},{40,64},{48,72},{56,80},{64,... | collective-permute-start | bytes 393224 | tf_op jit(solution)/shard_map/ppermute | solution.py:16
  100.2 23.3 %collective-permute-start.7 = (bf16[512,128]{1,0:T(8,128)(2,1)S(1)}, bf16[512,128]{1,0:T(8,128)(2,1)S(1)}, u32[]{:S(2)}, u32[]{:S(2)}) collective-permute-start(bf16[512,128]{1,0:T(8,128)(2,1)S(1)} %copy-done.2), channel_id=1, source_target_pairs={{16,0},{24,8},{32,16},{40,24},{48,32},{56,40},{64,48},{72,56},{80,... | collective-permute-start | bytes 393224 | tf_op jit(solution)/shard_map/ppermute | solution.py:16
  107.6 24.2 %collective-permute-start.5 = (bf16[512,128]{1,0:T(8,128)(2,1)S(1)}, bf16[512,128]{1,0:T(8,128)(2,1)S(1)}, u32[]{:S(2)}, u32[]{:S(2)}) collective-permute-start(bf16[512,128]{1,0:T(8,128)(2,1)S(1)} %copy-done.2), channel_id=1, source_target_pairs={{0,16},{8,24},{16,32},{24,40},{32,48},{40,56},{48,64},{56,72},{64,... | collective-permute-start | bytes 393224 | tf_op jit(solution)/shard_map/ppermute | solution.py:16
  110.0 24.2 %collective-permute-start.3 = (bf16[512,128]{1,0:T(8,128)(2,1)S(1)}, bf16[512,128]{1,0:T(8,128)(2,1)S(1)}, u32[]{:S(2)}, u32[]{:S(2)}) collective-permute-start(bf16[512,128]{1,0:T(8,128)(2,1)S(1)} %copy-done.2), channel_id=1, source_target_pairs={{8,0},{16,8},{24,16},{32,24},{40,32},{48,40},{56,48},{64,56},{72,6... | collective-permute-start | bytes 393224 | tf_op jit(solution)/shard_map/ppermute | solution.py:16
  115.9 25.1 %collective-permute-start.19 = (bf16[512,128]{1,0:T(8,128)(2,1)S(1)}, bf16[512,128]{1,0:T(8,128)(2,1)S(1)}, u32[]{:S(2)}, u32[]{:S(2)}) collective-permute-start(bf16[512,128]{1,0:T(8,128)(2,1)S(1)} %copy-done.2), channel_id=1, source_target_pairs={{40,0},{48,8},{56,16},{64,24},{72,32},{80,40},{88,48},{96,56},{104... | collective-permute-start | bytes 393224 | tf_op jit(solution)/shard_map/ppermute | solution.py:16
  121.1 22.5 %collective-permute-start.21 = (bf16[512,128]{1,0:T(8,128)(2,1)S(1)}, bf16[512,128]{1,0:T(8,128)(2,1)S(1)}, u32[]{:S(2)}, u32[]{:S(2)}) collective-permute-start(bf16[512,128]{1,0:T(8,128)(2,1)S(1)} %copy-done.2), channel_id=1, source_target_pairs={{0,48},{8,56},{16,64},{24,72},{32,80},{40,88},{48,96},{56,104},{64... | collective-permute-start | bytes 393224 | tf_op jit(solution)/shard_map/ppermute | solution.py:16
  123.5 20.6 %collective-permute-start.23 = (bf16[512,128]{1,0:T(8,128)(2,1)S(1)}, bf16[512,128]{1,0:T(8,128)(2,1)S(1)}, u32[]{:S(2)}, u32[]{:S(2)}) collective-permute-start(bf16[512,128]{1,0:T(8,128)(2,1)S(1)} %copy-done.2), channel_id=1, source_target_pairs={{48,0},{56,8},{64,16},{72,24},{80,32},{88,40},{96,48},{104,56},{11... | collective-permute-start | bytes 393224 | tf_op jit(solution)/shard_map/ppermute | solution.py:16
  131.8 12.8 %collective-permute-start.25 = (bf16[512,128]{1,0:T(8,128)(2,1)S(1)}, bf16[512,128]{1,0:T(8,128)(2,1)S(1)}, u32[]{:S(2)}, u32[]{:S(2)}) collective-permute-start(bf16[512,128]{1,0:T(8,128)(2,1)S(1)} %copy-done.2), channel_id=1, source_target_pairs={{0,56},{8,64},{16,72},{24,80},{32,88},{40,96},{48,104},{56,112},{6... | collective-permute-start | bytes 393224 | tf_op jit(solution)/shard_map/ppermute | solution.py:16
  134.2 10.9 %collective-permute-start.27 = (bf16[512,128]{1,0:T(8,128)(2,1)S(1)}, bf16[512,128]{1,0:T(8,128)(2,1)S(1)}, u32[]{:S(2)}, u32[]{:S(2)}) collective-permute-start(bf16[512,128]{1,0:T(8,128)(2,1)S(1)} %copy-done.2), channel_id=1, source_target_pairs={{56,0},{64,8},{72,16},{80,24},{88,32},{96,40},{104,48},{112,56},{1... | collective-permute-start | bytes 393224 | tf_op jit(solution)/shard_map/ppermute | solution.py:16
  141.0 9.0 %collective-permute-start.1 = (bf16[512,128]{1,0:T(8,128)(2,1)S(1)}, bf16[512,128]{1,0:T(8,128)(2,1)S(1)}, u32[]{:S(2)}, u32[]{:S(2)}) collective-permute-start(bf16[512,128]{1,0:T(8,128)(2,1)S(1)} %copy-done.2), channel_id=1, source_target_pairs={{0,8},{8,16},{16,24},{24,32},{32,40},{40,48},{48,56},{56,64},{64,7... | collective-permute-start | bytes 393224 | tf_op jit(solution)/shard_map/ppermute | solution.py:16
Sparse Core Ops, SparseCore 0:
  26.3 32.2 all-gather.1
where the time goes:
time: 173 us; the launch traced here: 172 us
  starting transfers between devices  110 us (64%)
  matrix products  17.2 us (10%)
  between operations  14.2 us (8%)
  blocking collectives  10.4 us (6%)
  other arithmetic  9.48 us (5%)
  local copies, waits for them, and re-layouts  5.87 us (3%)
  waiting for transfers between devices  4.51 us (3%)
    ppermute x28, starting transfers between devices, from_behind(): lax.ppermute(value, axis, [(source, source + steps) for source in range(f...  110 us
    all_to_all x1, blocking collectives, on_device(): lax.all_to_all(attended, 'head', split_axis=0, concat_axis=1, tiled=True)  10.4 us
    dot_general x15, matrix products, absorb(): jnp.einsum('hts,shd->htd', weights.astype(jnp.bfloat16), value_heads, pre...  7.69 us
    dot_general x15, matrix products, absorb(): jnp.einsum('thd,shd->hts', query_heads, key_heads, preferred_element_type...  6.25 us
    and x4, other arithmetic, block_mask(): return present & (inside | diagonal)  5.02 us
    ppermute x28, waiting for transfers between devices, from_behind(): lax.ppermute(value, axis, [(source, source + steps) for source in range(f...  4.49 us
    reduce_sum x15, other arithmetic, absorb(): totals = totals * rescale + jnp.sum(weights, axis=2)  4.36 us
  transfers between devices with their start and end apart: 29, of which 1 were waited for; matrix products, arithmetic and copies ran while one was open for 17% of the time, Pallas kernels for 0%

commit v1 on v0

v1 whole, which is shorter than its diff:
```python
import functools
import math

import jax
import jax.numpy as jnp
from jax import lax
from jax.experimental import pallas as pl
from jax.experimental.pallas import tpu as pltpu
from jax.sharding import PartitionSpec as P

RING = 4
HEADS = 8
HEAD = 128
BLK = 128
NB = 4
RADIUS = 7
ROWS = 64
PACKED = ROWS + 16
EXPONENT = math.log2(math.e) / math.sqrt(HEAD)
MESH = pl.DeviceIdType.MESH
BF16, F32 = jnp.bfloat16, jnp.float32


def turn(value, steps):
    return lax.rem(value + (RING + steps), RING)


def kernel(
    width_ref, offset_ref, q_hbm, k_hbm, v_hbm, w_hbm, out_ref,
    k_0, k_1, k_2, k_3, v_0, v_1, v_2, v_3, q_all, w_all,
    peak_ref, total_ref, mixed_ref, packed, arrived, attended,
    local_sem, kv_send, kv_recv, q_send, q_recv, w_send, w_recv, o_send, o_recv, self_sem,
):
    frame, head = lax.axis_index("frame"), lax.axis_index("head")
    x, z = lax.div(frame, RING), lax.rem(frame, RING)
    y, core = lax.div(head, 2), lax.rem(head, 2)

    def at(x, z, head):
        return (x * RING + z, head)

    x_next, x_last = at(turn(x, 1), z, head), at(turn(x, -1), z, head)
    z_next, z_last = at(x, turn(z, 1), head), at(x, turn(z, -1), head)
    head_next, head_last = turn(y, 1) * 2 + core, turn(y, -1) * 2 + core
    head_far, head_pair = turn(y, 2) * 2 + core, y * 2 + 1 - core
    y_next, y_last, pair = at(x, z, head_next), at(x, z, head_last), at(x, z, head_pair)

    def remote(source, target, send, recv, device):
        return pltpu.make_async_remote_copy(
            src_ref=source, dst_ref=target, send_sem=send, recv_sem=recv,
            device_id=device, device_id_type=MESH,
        )

    own = [
        pltpu.make_async_copy(q_hbm, q_all.at[0], local_sem.at[0]),
        pltpu.make_async_copy(k_hbm, k_0, local_sem.at[1]),
        pltpu.make_async_copy(v_hbm, v_0, local_sem.at[2]),
        pltpu.make_async_copy(w_hbm, w_all.at[head], local_sem.at[3]),
    ]
    for copy in own:
        copy.start()

    barrier = pltpu.get_barrier_semaphore()
    for device in (x_next, x_last):
        pl.semaphore_signal(barrier, inc=1, device_id=device, device_id_type=MESH)

    def greet(step, carry):
        other_z, other_head = lax.div(step, HEADS), lax.rem(step, HEADS)

        @pl.when((other_z != z) | (other_head != head))
        def _():
            pl.semaphore_signal(
                barrier, inc=1, device_id=at(x, other_z, other_head), device_id_type=MESH
            )

        return carry

    lax.fori_loop(0, RING * HEADS, greet, 0)
    pl.semaphore_wait(barrier, RING * HEADS + 1)

    kv = [
        remote(k_hbm, k_1, kv_send.at[0], kv_recv.at[0], x_next),
        remote(v_hbm, v_3, kv_send.at[1], kv_recv.at[1], x_last),
        remote(v_hbm, v_1, kv_send.at[2], kv_recv.at[2], x_next),
        remote(k_hbm, k_3, kv_send.at[3], kv_recv.at[3], x_last),
        remote(k_1, k_2, kv_send.at[4], kv_recv.at[4], x_next),
        remote(v_3, v_2, kv_send.at[5], kv_recv.at[5], x_last),
    ]
    low, high = pl.ds(0, NB // 2), pl.ds(NB // 2, NB // 2)
    qs = [
        remote(q_hbm.at[low], q_all.at[1, low], q_send.at[0], q_recv.at[0], z_next),
        remote(q_hbm.at[high], q_all.at[3, high], q_send.at[1], q_recv.at[1], z_last),
        remote(q_hbm.at[high], q_all.at[1, high], q_send.at[2], q_recv.at[2], z_next),
        remote(q_hbm.at[low], q_all.at[3, low], q_send.at[3], q_recv.at[3], z_last),
        remote(q_all.at[1, low], q_all.at[2, low], q_send.at[4], q_recv.at[4], z_next),
        remote(q_all.at[3, high], q_all.at[2, high], q_send.at[5], q_recv.at[5], z_last),
    ]
    top, end = pl.ds(0, HEAD // 2), pl.ds(HEAD // 2, HEAD // 2)
    ws = [
        remote(w_hbm.at[top], w_all.at[head, top], w_send.at[0], w_recv.at[0], y_next),
        remote(w_hbm.at[end], w_all.at[head, end], w_send.at[1], w_recv.at[1], y_last),
        remote(w_hbm.at[end], w_all.at[head, end], w_send.at[2], w_recv.at[2], y_next),
        remote(w_hbm.at[top], w_all.at[head, top], w_send.at[3], w_recv.at[3], y_last),
        remote(w_all.at[head_last, top], w_all.at[head_last, top], w_send.at[4], w_recv.at[4], y_next),
        remote(w_all.at[head_next, end], w_all.at[head_next, end], w_send.at[5], w_recv.at[5], y_last),
        remote(w_hbm, w_all.at[head], w_send.at[6], w_recv.at[6], pair),
        remote(w_all.at[head_last], w_all.at[head_last], w_send.at[7], w_recv.at[7], pair),
        remote(w_all.at[head_next], w_all.at[head_next], w_send.at[8], w_recv.at[8], pair),
        remote(w_all.at[head_far], w_all.at[head_far], w_send.at[9], w_recv.at[9], pair),
    ]
    for step in range(4):
        qs[step].start()
        kv[step].start()
    for step in range(4):
        ws[step].start()
    ws[6].start()

    ones = jnp.ones((BLK, HEAD), BF16)

    def query_frame(slot):
        return x * RING + turn(z, -slot)

    def gap(slot, key_frame):
        this = query_frame(slot)
        return jnp.maximum(this - key_frame, key_frame - this)

    def absorb(first, slot, block, scores, value_rows):
        rows = pl.ds(block * BLK, BLK)
        peak = jnp.max(functools.reduce(jnp.maximum, scores), axis=1, keepdims=True)
        if not first:
            before = peak_ref[slot, rows, :]
            peak = jnp.maximum(before, peak)
            keep = jnp.exp2((before - peak) * EXPONENT)
        weights = [jnp.exp2((part - peak) * EXPONENT).astype(BF16) for part in scores]
        weights = jnp.concatenate(weights, axis=1) if len(weights) > 1 else weights[0]
        extended = jnp.concatenate(
            [value_rows, jnp.concatenate([ones] * len(scores), axis=0)], axis=1
        )
        update = jnp.dot(weights, extended, preferred_element_type=F32)
        mixed, total = update[:, :HEAD], update[:, HEAD:]
        if not first:
            mixed += mixed_ref[slot, rows, :] * keep
            total += total_ref[slot, rows, :] * keep
        peak_ref[slot, rows, :] = jnp.broadcast_to(peak, (BLK, HEAD))
        mixed_ref[slot, rows, :] = mixed
        total_ref[slot, rows, :] = total

    def times(query_rows, key_rows):
        return lax.dot_general(
            query_rows, key_rows, (((1,), (1,)), ((), ())), preferred_element_type=F32
        )

    def query_rows(slot, block):
        return q_all[slot, block]

    def wide(first, slot, distance, k_ref, v_ref):
        this = query_frame(slot)
        span = width_ref[distance, this]
        tokens = NB * BLK
        keys, values = k_ref[...].reshape(tokens, HEAD), v_ref[...].reshape(tokens, HEAD)
        key_block = lax.broadcasted_iota(jnp.int32, (1, tokens), 1) // BLK
        for block in range(NB):
            scores = times(query_rows(slot, block), keys)
            past = lax.rem(key_block + (NB - offset_ref[distance, block, this]), NB)
            diagonal = key_block == jnp.where(distance == 0, block, NB)
            scores += jnp.where((past < span) | diagonal, 0.0, -1e30)
            parts = [scores[:, other * BLK:(other + 1) * BLK] for other in range(NB)]
            absorb(first, slot, block, parts, values)

    def narrow(first, slot, distance, k_ref, v_ref, count):
        this = query_frame(slot)
        for block in range(NB):
            offset = offset_ref[distance, block, this]
            keys, values = [], []
            for step in range(count):
                chosen = lax.rem(offset + step, NB)
                keys.append(k_ref[chosen])
                values.append(v_ref[chosen])
            if count > 1:
                keys, values = [jnp.concatenate(keys, axis=0)], [jnp.concatenate(values, axis=0)]
            scores = times(query_rows(slot, block), keys[0])
            parts = [scores[:, step * BLK:(step + 1) * BLK] for step in range(count)]
            absorb(first, slot, block, parts, values[0])

    def take(first, slot, key_frame, k_ref, v_ref, singles):
        distance = gap(slot, key_frame)

        @pl.when(distance <= 1)
        def _():
            wide(first, slot, distance, k_ref, v_ref)

        @pl.when((distance >= 2) & (distance <= 3))
        def _():
            narrow(first, slot, distance, k_ref, v_ref, 2)

        if singles:

            @pl.when((distance >= 4) & (distance <= RADIUS))
            def _():
                narrow(first, slot, distance, k_ref, v_ref, 1)

    qs[0].wait_recv()
    qs[4].start()
    qs[1].wait_recv()
    qs[5].start()
    for copy in own[:3]:
        copy.wait()
    kv[0].wait_recv()
    kv[4].start()
    kv[1].wait_recv()
    kv[5].start()
    ws[0].wait_recv()
    ws[4].start()
    ws[1].wait_recv()
    ws[5].start()
    for step in range(2, 6):
        qs[step].wait_recv()

    def stage(first, steps, k_ref, v_ref):
        key_frame = turn(x, steps) * RING + z

        def each(slot, carry):
            take(first, slot, key_frame, k_ref, v_ref, not first)
            return carry

        lax.fori_loop(0, RING, each, 0)

    stage(True, 0, k_0, v_0)
    kv[2].wait_recv()
    stage(False, -1, k_1, v_1)
    kv[3].wait_recv()
    stage(False, 1, k_3, v_3)

    ws[2].wait_recv()
    ws[7].start()
    ws[3].wait_recv()
    ws[8].start()

    far_frame = turn(x, 2) * RING + z
    row = lax.broadcasted_iota(jnp.int32, (BLK, BLK), 0)
    lane = lax.broadcasted_iota(jnp.int32, (BLK, BLK), 1)
    small_row = lax.broadcasted_iota(jnp.int32, (16, BLK), 0)

    def share(slot, receiver):
        return packed.at[slot, receiver], arrived.at[head, z]

    def finish(slot):
        for block in range(NB):
            rows = pl.ds(block * BLK, BLK)
            total = total_ref[slot, rows, :]
            scaled = (mixed_ref[slot, rows, :] / total).astype(BF16)
            level = peak_ref[slot, rows, :] * EXPONENT + jnp.log(total) * math.log2(math.e)
            level = jnp.sum(jnp.where(row == lane, level, 0.0), axis=0, keepdims=True)
            high_part = level.astype(BF16).astype(F32)
            rest = level - high_part
            mid_part = rest.astype(BF16).astype(F32)
            tile = jnp.where(
                small_row == 0, high_part,
                jnp.where(small_row == 1, mid_part, jnp.where(small_row == 2, rest - mid_part, 0.0)),
            ).astype(BF16)
            for half in range(2):
                packed[slot, 2 * block + half, 0:ROWS, :] = scaled[half * ROWS:(half + 1) * ROWS]
                packed[slot, 2 * block + half, ROWS:PACKED, :] = tile

        def send(receiver, carry):
            source, target = share(slot, receiver)
            here = (slot == 0) & (receiver == head)

            @pl.when(here)
            def _():
                pltpu.make_async_copy(source, target, self_sem).start()

            @pl.when(jnp.logical_not(here))
            def _():
                remote(
                    source, target, o_send.at[slot], o_recv.at[head], at(x, turn(z, -slot), receiver)
                ).start()

            return carry

        lax.fori_loop(0, HEADS, send, 0)

    def closing(step, carry):
        late, turn_of = lax.div(step, RING), lax.rem(step, RING)
        slot = lax.rem(2 + 3 * turn_of + 3 * lax.div(turn_of, 2) + 2 * lax.div(turn_of, 3), RING)
        distance = gap(slot, far_frame)
        needs = distance <= RADIUS

        @pl.when(step == RING)
        def _():
            kv[4].wait_recv()
            kv[5].wait_recv()

        @pl.when((late == 0) & jnp.logical_not(needs))
        def _():
            finish(slot)

        @pl.when((late == 1) & needs)
        def _():
            narrow(False, slot, distance, k_2, v_2, 1)
            finish(slot)

        return carry

    lax.fori_loop(0, 2 * RING, closing, 0)

    ws[4].wait_recv()
    ws[5].wait_recv()
    ws[9].start()

    pltpu.make_async_copy(packed.at[0, head], arrived.at[head, z], self_sem).wait()
    column = lax.broadcasted_iota(jnp.int32, (ROWS, HEAD), 1)
    here = lax.broadcasted_iota(jnp.int32, (ROWS, HEAD), 0) + core * ROWS
    for other in range(HEADS):
        mine = other == head

        @pl.when(mine)
        def _():
            three = pltpu.make_async_copy(
                arrived.at[other, pl.ds(0, 3)], arrived.at[other, pl.ds(0, 3)], o_recv.at[other]
            )
            three.wait()

        @pl.when(jnp.logical_not(mine))
        def _():
            four = pltpu.make_async_copy(arrived.at[other], arrived.at[other], o_recv.at[other])
            four.wait()

    for other in range(HEADS):
        levels = []
        for part in range(RING):
            tile = arrived[other, part, ROWS:PACKED, :].astype(F32)
            levels.append(jnp.sum(tile, axis=0, keepdims=True))
        peak = functools.reduce(jnp.maximum, levels)
        shares = [jnp.exp2(level - peak) for level in levels]
        whole = functools.reduce(jnp.add, shares)
        merged = jnp.zeros((ROWS, HEAD), F32)
        for part in range(RING):
            share_row = shares[part] / whole
            share_column = jnp.sum(
                jnp.where(column == here, jnp.broadcast_to(share_row, (ROWS, HEAD)), 0.0),
                axis=1, keepdims=True,
            )
            merged += arrived[other, part, 0:ROWS, :].astype(F32) * share_column
        attended[:, other * HEAD:(other + 1) * HEAD] = merged.astype(BF16)

    own[3].wait()
    for step in range(6, 10):
        ws[step].wait_recv()
    depth, columns = HEADS * HEAD, w_all.shape[2]
    tile = 512
    for start in range(0, columns, tile):
        weight = w_all[:, :, start:start + tile].reshape(depth, tile)
        out_ref[:, start:start + tile] = jnp.dot(
            attended[...], weight, preferred_element_type=F32
        ).astype(BF16)

    for copy in kv + qs + ws:
        copy.wait_send()
    seven = packed.at[0, pl.ds(0, HEADS - 1)]
    pltpu.make_async_copy(seven, seven, o_send.at[0]).wait()
    for slot in range(1, RING):
        pltpu.make_async_copy(packed.at[slot], packed.at[slot], o_send.at[slot]).wait()


def on_device(queries, keys, values, band_width, band_offset, out_weight):
    tokens, width = queries.shape[0], out_weight.shape[1]
    queries, keys, values = (array.reshape(NB, BLK, HEAD) for array in (queries, keys, values))
    band_width, band_offset = band_width.T, band_offset.transpose(1, 2, 0)
    block = pltpu.VMEM((NB, BLK, HEAD), BF16)
    state = pltpu.VMEM((RING, tokens, HEAD), F32)
    dma = pltpu.SemaphoreType.DMA
    smem, anywhere = pl.BlockSpec(memory_space=pltpu.SMEM), pl.BlockSpec(memory_space=pltpu.HBM)
    return pl.pallas_call(
        kernel,
        out_shape=jax.ShapeDtypeStruct((ROWS, width), BF16),
        in_specs=[smem, smem] + [anywhere] * 4,
        out_specs=pl.BlockSpec(memory_space=pltpu.VMEM),
        scratch_shapes=[block] * 8
        + [
            pltpu.VMEM((RING, NB, BLK, HEAD), BF16),
            pltpu.VMEM((HEADS, HEAD, width), BF16),
            state, state, state,
            pltpu.VMEM((RING, HEADS, PACKED, HEAD), BF16),
            pltpu.VMEM((HEADS, RING, PACKED, HEAD), BF16),
            pltpu.VMEM((ROWS, HEADS * HEAD), BF16),
            dma((4,)), dma((6,)), dma((6,)), dma((6,)), dma((6,)), dma((10,)), dma((10,)),
            dma((RING,)), dma((HEADS,)), dma,
        ],
        compiler_params=pltpu.CompilerParams(
            collective_id=0, has_side_effects=True, vmem_limit_bytes=64 * 1024 * 1024
        ),
    )(band_width, band_offset, queries, keys, values, out_weight)


def solution(mesh):
    placed = (P("frame", "head"), P("frame", "head"), P("frame", "head"), P(), P(), P("head", None))
    return jax.shard_map(
        on_device, mesh=mesh, in_specs=placed, out_specs=P(("frame", "head"), None), check_vma=False
    )
```

time: 173 us -> 40.7 us (0.24)
  the two profiles are of different devices: /device:TPU:4 before, /device:TPU:5 now
where the time goes in v1:
time: 40.7 us; the launch traced here: 40.5 us
  Pallas kernels  38.8 us (95%)
  local copies, waits for them, and re-layouts  1.62 us (4%)
    pallas_call x1, Pallas kernels, on_device(): pl.pallas_call(kernel, out_shape=jax.ShapeDtypeStruct((ROWS, width), BF16...  38.8 us
    unnamed x1, local copies, waits for them, and re-layouts  1.62 us

profile of v1, /device:TPU:5, one launch (start us, length us, event | category | flops | bytes accessed | tf_op | source)
XLA Modules:
  0.0 40.5 jit_solution(9454683293681400461)
XLA Ops:
  0.0 38.8 %shard_map.64 = bf16[64,1536]{1,0:T(8,128)(2,1)} custom-call(s32[8,16]{1,0:T(8,128)} %bitcast.9, s32[8,4,16]{2,1,0:T(4,128)} %bitcast.8, bf16[4,128,128]{2,1,0:T(8,128)(2,1)} %bitcast.5, bf16[4,128,128]{2,1,0:T(8,128)(2,1)} %bitcast.6, bf16[4,128,128]{2,1,0:T(8,128)(2,1)} %bitcast.7, bf16[128,1536]{1,0:T(8,128)(2,1)} %w_hbm.1), custom_call_target="tpu_custom_call" | custom-call | tf_op jit(solution)/shard_map/pallas_call | solution.py:373
  38.9 1.6 %copy.8 = bf16[64,1536]{1,0:T(8,128)(2,1)} copy(bf16[64,1536]{1,0:T(8,128)(2,1)} %shard_map.64) | data formatting | bytes 393216

commit v2 on v0

v2 whole, which is shorter than its diff:
```python
import functools
import math

import jax
import jax.numpy as jnp
from jax import lax
from jax.experimental import pallas as pl
from jax.experimental.pallas import tpu as pltpu
from jax.sharding import PartitionSpec as P

RING = 4
HEADS = 8
HEAD = 128
BLK = 128
NB = 4
RADIUS = 7
ROWS = 64
HALF = NB // 2
PACKED = HALF * BLK + 16
LOG2E = math.log2(math.e)
EXPONENT = LOG2E / math.sqrt(HEAD)
LOW = -1e30
MESH = pl.DeviceIdType.MESH
BF16, F32 = jnp.bfloat16, jnp.float32


def turn(value, steps):
    return lax.rem(value + (RING + steps), RING)


def kernel(
    width_ref, offset_ref, q_hbm, k_hbm, v_hbm, w_hbm, out_ref,
    k_0, k_1, k_2, k_3, v_0, v_1, v_2, v_3, q_all, w_all,
    peak_ref, total_ref, mixed_ref, packed, passing, arrived, rows_out, rows_in, sums,
    local_sem, kv_send, kv_recv, q_send, q_recv, w_send, w_recv, o_send, o_recv, a_send, a_recv,
):
    frame, head = lax.axis_index("frame"), lax.axis_index("head")
    x, z = lax.div(frame, RING), lax.rem(frame, RING)
    y, core = lax.div(head, 2), lax.rem(head, 2)

    def at(x, z, head):
        return (x * RING + z, head)

    x_next, x_last = at(turn(x, 1), z, head), at(turn(x, -1), z, head)
    z_next, z_last = at(x, turn(z, 1), head), at(x, turn(z, -1), head)
    head_next, head_last = turn(y, 1) * 2 + core, turn(y, -1) * 2 + core
    head_far, head_pair = turn(y, 2) * 2 + core, y * 2 + 1 - core
    y_next, y_last, pair = at(x, z, head_next), at(x, z, head_last), at(x, z, head_pair)
    others = [turn(y, step) * 2 + lax.rem(core + side, 2) for step in (2, 1, -1) for side in (0, 1)]
    others.append(head_pair)

    def remote(source, target, send, recv, device):
        return pltpu.make_async_remote_copy(
            src_ref=source, dst_ref=target, send_sem=send, recv_sem=recv,
            device_id=device, device_id_type=MESH,
        )

    barrier = pltpu.get_barrier_semaphore()
    greeted = [at(x, z, other) for other in others] + [x_next, x_last, z_next, z_last]
    for device in greeted:
        pl.semaphore_signal(barrier, inc=1, device_id=device, device_id_type=MESH)

    own = [
        pltpu.make_async_copy(q_hbm, q_all.at[0], local_sem.at[0]),
        pltpu.make_async_copy(k_hbm, k_0, local_sem.at[1]),
        pltpu.make_async_copy(v_hbm, v_0, local_sem.at[2]),
        pltpu.make_async_copy(w_hbm, w_all.at[head], local_sem.at[3]),
    ]
    for copy in own:
        copy.start()
    pl.semaphore_wait(barrier, len(greeted))

    kv = [
        remote(k_hbm, k_1, kv_send.at[0], kv_recv.at[0], x_next),
        remote(v_hbm, v_3, kv_send.at[1], kv_recv.at[1], x_last),
        remote(v_hbm, v_1, kv_send.at[2], kv_recv.at[2], x_next),
        remote(k_hbm, k_3, kv_send.at[3], kv_recv.at[3], x_last),
        remote(k_1, k_2, kv_send.at[4], kv_recv.at[4], x_next),
        remote(v_3, v_2, kv_send.at[5], kv_recv.at[5], x_last),
    ]
    low, high = pl.ds(0, HALF), pl.ds(HALF, HALF)
    qs = [
        remote(q_hbm.at[low], q_all.at[1, low], q_send.at[0], q_recv.at[0], z_next),
        remote(q_hbm.at[high], q_all.at[3, high], q_send.at[1], q_recv.at[1], z_last),
        remote(q_hbm.at[high], q_all.at[1, high], q_send.at[2], q_recv.at[2], z_next),
        remote(q_hbm.at[low], q_all.at[3, low], q_send.at[3], q_recv.at[3], z_last),
        remote(q_all.at[1, low], q_all.at[2, low], q_send.at[4], q_recv.at[4], z_next),
        remote(q_all.at[3, high], q_all.at[2, high], q_send.at[5], q_recv.at[5], z_last),
    ]
    top, end = pl.ds(0, HEAD // 2), pl.ds(HEAD // 2, HEAD // 2)
    ws = [
        remote(w_hbm.at[top], w_all.at[head, top], w_send.at[0], w_recv.at[0], y_next),
        remote(w_hbm.at[end], w_all.at[head, end], w_send.at[1], w_recv.at[1], y_last),
        remote(w_hbm.at[end], w_all.at[head, end], w_send.at[2], w_recv.at[2], y_next),
        remote(w_hbm.at[top], w_all.at[head, top], w_send.at[3], w_recv.at[3], y_last),
        remote(w_all.at[head_last, top], w_all.at[head_last, top], w_send.at[4], w_recv.at[4], y_next),
        remote(w_all.at[head_next, end], w_all.at[head_next, end], w_send.at[5], w_recv.at[5], y_last),
        remote(w_hbm, w_all.at[head], w_send.at[6], w_recv.at[6], pair),
        remote(w_all.at[head_last], w_all.at[head_last], w_send.at[7], w_recv.at[7], pair),
        remote(w_all.at[head_next], w_all.at[head_next], w_send.at[8], w_recv.at[8], pair),
        remote(w_all.at[head_far], w_all.at[head_far], w_send.at[9], w_recv.at[9], pair),
    ]
    os = [
        remote(packed.at[2, 0], passing.at[0], o_send.at[0], o_recv.at[0], z_next),
        remote(packed.at[2, 1], passing.at[1], o_send.at[1], o_recv.at[1], z_last),
        remote(packed.at[3], arrived.at[0], o_send.at[2], o_recv.at[2], z_next),
        remote(packed.at[1], arrived.at[1], o_send.at[3], o_recv.at[3], z_last),
        remote(passing.at[0], arrived.at[2, 0], o_send.at[4], o_recv.at[4], z_next),
        remote(passing.at[1], arrived.at[2, 1], o_send.at[5], o_recv.at[5], z_last),
    ]
    for step in range(4):
        kv[step].start()
        qs[step].start()
    for step in range(4):
        ws[step].start()
    ws[6].start()

    ones = jnp.ones((BLK, HEAD), BF16)
    tokens = NB * BLK
    key_block = lax.broadcasted_iota(jnp.int32, (1, tokens), 1) // BLK

    def query_frame(slot):
        return x * RING + turn(z, -slot)

    def wide(slot, distance, k_ref, v_ref, valid):
        this = query_frame(slot)

        def pick(block):
            past = lax.rem(key_block + (NB - offset_ref[distance, block, this]), NB)
            inside = past < width_ref[distance, this]
            inside = inside | (key_block == jnp.where(distance == 0, block, NB))
            added = jnp.where(inside, 0.0, LOW)
            if valid is not None:
                added += jnp.where(valid, 0.0, LOW)
            return k_ref[...].reshape(tokens, HEAD), v_ref[...].reshape(tokens, HEAD), added

        return NB, pick

    def narrow(slot, distance, k_ref, v_ref, valid, count):
        this = query_frame(slot)

        def pick(block):
            offset = offset_ref[distance, block, this]
            chosen = [lax.rem(offset + step, NB) for step in range(count)]
            keys, values = [k_ref[index] for index in chosen], [v_ref[index] for index in chosen]
            if count > 1:
                keys, values = [jnp.concatenate(keys, axis=0)], [jnp.concatenate(values, axis=0)]
            return keys[0], values[0], None if valid is None else jnp.where(valid, 0.0, LOW)

        return count, pick

    def join(pieces):
        return pieces[0] if len(pieces) == 1 else jnp.concatenate(pieces, axis=0)

    def attend(slot, sources, first, blocks):
        count = sum(source[0] for source in sources)
        states, scores, values = [], [], []
        for block in blocks:
            picked = [source[1](block) for source in sources]
            full = lax.dot_general(
                q_all[slot, block], join([keys for keys, _, _ in picked]), (((1,), (1,)), ((), ())),
                preferred_element_type=F32,
            )
            parts = [full[:, step * BLK:(step + 1) * BLK] for step in range(count)]
            begin = 0
            for (size, _), (_, _, added) in zip(sources, picked):
                for step in range(size):
                    if added is not None:
                        more = added[:, step * BLK:(step + 1) * BLK] if added.ndim else added
                        parts[begin + step] += more
                begin += size
            scores.append(parts)
            values.append(join([rows for _, rows, _ in picked]))
        keeps, peaks = [], []
        for block, parts in zip(blocks, scores):
            peak = jnp.max(functools.reduce(jnp.maximum, parts), axis=1, keepdims=True)
            if not first:
                before = peak_ref[slot, block]
                peak = jnp.maximum(before, peak)
                keeps.append(jnp.exp2((before - peak) * EXPONENT))
            peaks.append(peak)
        updates = []
        for parts, peak, rows in zip(scores, peaks, values):
            weights = [jnp.exp2((part - peak) * EXPONENT).astype(BF16) for part in parts]
            weights = weights[0] if count == 1 else jnp.concatenate(weights, axis=1)
            extended = jnp.concatenate([rows, join([ones] * count)], axis=1)
            updates.append(jnp.dot(weights, extended, preferred_element_type=F32))
        for index, block in enumerate(blocks):
            mixed, total = updates[index][:, :HEAD], updates[index][:, HEAD:]
            if not first:
                mixed += mixed_ref[slot, block] * keeps[index]
                total += total_ref[slot, block] * keeps[index]
            states.append((jnp.broadcast_to(peaks[index], (BLK, HEAD)), total, mixed))
        return states

    def keep(slot, states, blocks):
        for block, (peak, total, mixed) in zip(blocks, states):
            peak_ref[slot, block] = peak
            total_ref[slot, block] = total
            mixed_ref[slot, block] = mixed

    def absorb(slot, sources, first, group):
        for begin in range(0, NB, group):
            blocks = range(begin, begin + group)
            keep(slot, attend(slot, sources, first, blocks), blocks)

    row = lax.broadcasted_iota(jnp.int32, (BLK, BLK), 0)
    lane = lax.broadcasted_iota(jnp.int32, (BLK, BLK), 1)
    small_row = lax.broadcasted_iota(jnp.int32, (16, BLK), 0)

    def pack(slot, states):
        tiles = []
        for block, (peak, total, mixed) in enumerate(states):
            packed[slot, block // HALF, pl.ds(block % HALF * BLK, BLK), :] = (mixed / total).astype(BF16)
            level = peak * EXPONENT + jnp.log(total) * LOG2E
            level = jnp.sum(jnp.where(row == lane, level, 0.0), axis=0, keepdims=True)
            first = level.astype(BF16).astype(F32)
            second = (level - first).astype(BF16).astype(F32)
            tiles.append((first, second, level - first - second))
        for half in range(HALF):
            tile = jnp.zeros((16, BLK), F32)
            for index in range(HALF):
                for term in range(3):
                    tile = jnp.where(small_row == term * HALF + index, tiles[half * HALF + index][term], tile)
            packed[slot, half, pl.ds(HALF * BLK, 16), :] = tile.astype(BF16)

    every = range(NB)
    qs[0].wait_recv()
    qs[4].start()
    qs[1].wait_recv()
    qs[5].start()
    for copy in own[:3]:
        copy.wait()

    def own_keys(step, carry):
        slot = step + lax.div(step, 2) - 2 * lax.div(step, 3)

        @pl.when(step == 1)
        def _():
            kv[0].wait_recv()
            kv[4].start()
            kv[1].wait_recv()
            kv[5].start()
            qs[2].wait_recv()
            qs[3].wait_recv()

        @pl.when(step == 3)
        def _():
            ws[0].wait_recv()
            ws[4].start()
            ws[1].wait_recv()
            ws[5].start()
            qs[4].wait_recv()
            qs[5].wait_recv()

        ahead = turn(z, -slot) - z
        distance = jnp.maximum(ahead, -ahead)

        @pl.when(distance <= 1)
        def _():
            absorb(slot, [wide(slot, distance, k_0, v_0, None)], True, 2)

        @pl.when(distance >= 2)
        def _():
            absorb(slot, [narrow(slot, distance, k_0, v_0, None, 2)], True, NB)

        return carry

    lax.fori_loop(0, RING, own_keys, 0)
    kv[2].wait_recv()
    kv[3].wait_recv()

    def near_keys(slot, carry):
        ahead = turn(z, -slot) - z
        distance = jnp.maximum(ahead, -ahead)
        last, next_ = (k_1, v_1, x >= 1), (k_3, v_3, x <= RING - 2)

        @pl.when(distance == 0)
        def _():
            absorb(slot, [narrow(slot, RING, *last, 1), narrow(slot, RING, *next_, 1)], False, NB)

        for sign, near, far in ((1, next_, last), (-1, last, next_)):

            @pl.when((ahead * sign >= 1) & (ahead * sign <= 2))
            def _():
                absorb(
                    slot,
                    [
                        narrow(slot, RING - distance, *near, 2),
                        narrow(slot, RING + distance, *far, 1),
                    ],
                    False, NB,
                )

            @pl.when(ahead * sign == 3)
            def _():
                absorb(slot, [wide(slot, 1, *near), narrow(slot, RADIUS, *far, 1)], False, 2)

        return carry

    lax.fori_loop(0, RING, near_keys, 0)

    far_frame = turn(x, 2) * RING + z

    def closing(step, carry):
        late, place = lax.div(step, RING - 1), lax.rem(step, RING - 1)
        slot = lax.rem(2 + place + lax.div(place, 2), RING)
        this = query_frame(slot)
        distance = jnp.maximum(this - far_frame, far_frame - this)
        needs = distance <= RADIUS

        @pl.when(step == RING - 1)
        def _():
            kv[4].wait_recv()
            kv[5].wait_recv()

        @pl.when((late == 0) & jnp.logical_not(needs))
        def _():
            pack(slot, [(peak_ref[slot, b], total_ref[slot, b], mixed_ref[slot, b]) for b in every])

        @pl.when((late == 1) & needs)
        def _():
            pack(slot, attend(slot, [narrow(slot, distance, k_2, v_2, None, 1)], False, every))

        done = needs == (late == 1)

        @pl.when(done & (slot == 2))
        def _():
            os[0].start()
            os[1].start()

        @pl.when(done & (slot == 3))
        def _():
            os[2].start()

        @pl.when(done & (slot == 1))
        def _():
            os[3].start()

        return carry

    lax.fori_loop(0, 2 * (RING - 1), closing, 0)
    os[0].wait_recv()
    os[4].start()
    os[1].wait_recv()
    os[5].start()
    ws[2].wait_recv()
    ws[7].start()
    ws[3].wait_recv()
    ws[8].start()
    for step in range(2, 6):
        os[step].wait_recv()

    for block in every:
        half, place = block // HALF, block % HALF
        peak, total, mixed = peak_ref[0, block] * EXPONENT, total_ref[0, block], mixed_ref[0, block]
        levels = []
        for part in range(RING - 1):
            tile = arrived[part, half, pl.ds(HALF * BLK, 16), :].astype(F32)
            level = jnp.sum(jnp.where(lax.rem(small_row, HALF) == place, tile, 0.0), axis=0, keepdims=True)
            level = jnp.where(row == lane, jnp.broadcast_to(level, (BLK, BLK)), 0.0)
            levels.append(jnp.sum(level, axis=1, keepdims=True))
        top_level = jnp.maximum(functools.reduce(jnp.maximum, levels), peak)
        share = jnp.exp2(peak - top_level)
        total, mixed = total * share, mixed * share
        for part in range(RING - 1):
            share = jnp.exp2(levels[part] - top_level)
            total += share
            mixed += arrived[part, half, pl.ds(place * BLK, BLK), :].astype(F32) * share
        merged = (mixed / total).astype(BF16)
        rows_out[2 * block] = merged[:ROWS]
        rows_out[2 * block + 1] = merged[ROWS:]

    mine = pltpu.make_async_copy(rows_out.at[head], rows_in.at[head], local_sem.at[4])
    to_heads = [
        remote(rows_out.at[other], rows_in.at[head], a_send.at[index], a_recv.at[head], at(x, z, other))
        for index, other in enumerate(others)
    ]
    for copy in to_heads:
        copy.start()
    mine.start()

    ws[4].wait_recv()
    ws[5].wait_recv()
    ws[9].start()
    own[3].wait()
    mine.wait()
    for step in range(6, 9):
        ws[step].wait_recv()

    columns, tile = w_all.shape[2], 512
    for index, step in enumerate((0, -1, 1, 2)):
        chip = turn(y, step)
        if step == 2:
            ws[9].wait_recv()
        for side in range(2):
            other = chip * 2 + side

            @pl.when(other != head)
            def _():
                pltpu.make_async_copy(rows_in.at[other], rows_in.at[other], a_recv.at[other]).wait()

        left = jnp.concatenate([rows_in[chip * 2], rows_in[chip * 2 + 1]], axis=1)
        for start in range(0, columns, tile):
            weight = w_all[pl.ds(chip * 2, 2), :, start:start + tile].reshape(2 * HEAD, tile)
            term = jnp.dot(left, weight, preferred_element_type=F32)
            if index > 0:
                term += sums[:, start:start + tile]
            if index < RING - 1:
                sums[:, start:start + tile] = term
            else:
                out_ref[:, start:start + tile] = term.astype(BF16)

    for copy in kv + qs + ws + os + to_heads:
        copy.wait_send()


def on_device(queries, keys, values, band_width, band_offset, out_weight):
    width = out_weight.shape[1]
    queries, keys, values = (array.reshape(NB, BLK, HEAD) for array in (queries, keys, values))
    band_width, band_offset = band_width.T, band_offset.transpose(1, 2, 0)
    block = pltpu.VMEM((NB, BLK, HEAD), BF16)
    state = pltpu.VMEM((RING, NB, BLK, HEAD), F32)
    dma = pltpu.SemaphoreType.DMA
    smem, anywhere = pl.BlockSpec(memory_space=pltpu.SMEM), pl.BlockSpec(memory_space=pltpu.HBM)
    return pl.pallas_call(
        kernel,
        out_shape=jax.ShapeDtypeStruct((ROWS, width), BF16),
        in_specs=[smem, smem] + [anywhere] * 4,
        out_specs=pl.BlockSpec(memory_space=pltpu.VMEM),
        scratch_shapes=[block] * 8
        + [
            pltpu.VMEM((RING, NB, BLK, HEAD), BF16),
            pltpu.VMEM((HEADS, HEAD, width), BF16),
            state, state, state,
            pltpu.VMEM((RING, 2, PACKED, HEAD), BF16),
            pltpu.VMEM((2, PACKED, HEAD), BF16),
            pltpu.VMEM((RING - 1, 2, PACKED, HEAD), BF16),
            pltpu.VMEM((HEADS, ROWS, HEAD), BF16),
            pltpu.VMEM((HEADS, ROWS, HEAD), BF16),
            pltpu.VMEM((ROWS, width), F32),
            dma((5,)), dma((6,)), dma((6,)), dma((6,)), dma((6,)), dma((10,)), dma((10,)),
            dma((6,)), dma((6,)), dma((HEADS - 1,)), dma((HEADS,)),
        ],
        compiler_params=pltpu.CompilerParams(
            collective_id=0, has_side_effects=True, vmem_limit_bytes=64 * 1024 * 1024
        ),
    )(band_width, band_offset, queries, keys, values, out_weight)


def solution(mesh):
    placed = (P("frame", "head"), P("frame", "head"), P("frame", "head"), P(), P(), P("head", None))
    return jax.shard_map(
        on_device, mesh=mesh, in_specs=placed, out_specs=P(("frame", "head"), None), check_vma=False
    )
```

time: 173 us -> 36 us (0.21)
  the two profiles are of different devices: /device:TPU:4 before, /device:TPU:1 now
where the time goes in v2:
time: 36 us; the launch traced here: 35.7 us
  Pallas kernels  34.1 us (95%)
  local copies, waits for them, and re-layouts  1.62 us (4%)
    pallas_call x1, Pallas kernels, on_device(): pl.pallas_call(kernel, out_shape=jax.ShapeDtypeStruct((ROWS, width), BF16...  34.1 us
    unnamed x1, local copies, waits for them, and re-layouts  1.62 us

profile of v2, /device:TPU:1, one launch (start us, length us, event | category | flops | bytes accessed | tf_op | source)
XLA Modules:
  0.0 35.7 jit_solution(5853087054658477400)
XLA Ops:
  0.0 34.1 %shard_map.64 = bf16[64,1536]{1,0:T(8,128)(2,1)} custom-call(s32[8,16]{1,0:T(8,128)} %bitcast.9, s32[8,4,16]{2,1,0:T(4,128)} %bitcast.8, bf16[4,128,128]{2,1,0:T(8,128)(2,1)} %bitcast.5, bf16[4,128,128]{2,1,0:T(8,128)(2,1)} %bitcast.6, bf16[4,128,128]{2,1,0:T(8,128)(2,1)} %bitcast.7, bf16[128,1536]{1,0:T(8,128)(2,1)} %w_hbm.1), custom_call_target="tpu_custom_call" | custom-call | tf_op jit(solution)/shard_map/pallas_call | solution.py:426
  34.1 1.6 %copy.8 = bf16[64,1536]{1,0:T(8,128)(2,1)} copy(bf16[64,1536]{1,0:T(8,128)(2,1)} %shard_map.64) | data formatting | bytes 393216

commit v3 on v2

--- a/solution.py
+++ b/solution.py
@@ -16,7 +16,7 @@
 RADIUS = 7
 ROWS = 64
 HALF = NB // 2
-PACKED = HALF * BLK + 16
+PACKED = ROWS + 16
 LOG2E = math.log2(math.e)
 EXPONENT = LOG2E / math.sqrt(HEAD)
 LOW = -1e30
@@ -31,8 +31,8 @@
 def kernel(
     width_ref, offset_ref, q_hbm, k_hbm, v_hbm, w_hbm, out_ref,
     k_0, k_1, k_2, k_3, v_0, v_1, v_2, v_3, q_all, w_all,
-    peak_ref, total_ref, mixed_ref, packed, passing, arrived, rows_out, rows_in, sums,
-    local_sem, kv_send, kv_recv, q_send, q_recv, w_send, w_recv, o_send, o_recv, a_send, a_recv,
+    peak_ref, total_ref, mixed_ref, packed, arrived, sums,
+    local_sem, kv_send, kv_recv, q_send, q_recv, w_send, w_recv, o_send, o_recv, ready,
 ):
     frame, head = lax.axis_index("frame"), lax.axis_index("head")
     x, z = lax.div(frame, RING), lax.rem(frame, RING)
@@ -46,9 +46,6 @@
     head_next, head_last = turn(y, 1) * 2 + core, turn(y, -1) * 2 + core
     head_far, head_pair = turn(y, 2) * 2 + core, y * 2 + 1 - core
     y_next, y_last, pair = at(x, z, head_next), at(x, z, head_last), at(x, z, head_pair)
-    others = [turn(y, step) * 2 + lax.rem(core + side, 2) for step in (2, 1, -1) for side in (0, 1)]
-    others.append(head_pair)
-
     def remote(source, target, send, recv, device):
         return pltpu.make_async_remote_copy(
             src_ref=source, dst_ref=target, send_sem=send, recv_sem=recv,
@@ -56,9 +53,13 @@
         )
 
     barrier = pltpu.get_barrier_semaphore()
-    greeted = [at(x, z, other) for other in others] + [x_next, x_last, z_next, z_last]
+    greeted = [x_next, x_last, z_next, z_last, y_next, y_last, pair]
     for device in greeted:
         pl.semaphore_signal(barrier, inc=1, device_id=device, device_id_type=MESH)
+
+    def announce(turn_, devices):
+        for device in devices:
+            pl.semaphore_signal(ready.at[turn_], inc=1, device_id=device, device_id_type=MESH)
 
     own = [
         pltpu.make_async_copy(q_hbm, q_all.at[0], local_sem.at[0]),
@@ -100,20 +101,13 @@
         remote(w_all.at[head_next], w_all.at[head_next], w_send.at[8], w_recv.at[8], pair),
         remote(w_all.at[head_far], w_all.at[head_far], w_send.at[9], w_recv.at[9], pair),
     ]
-    os = [
-        remote(packed.at[2, 0], passing.at[0], o_send.at[0], o_recv.at[0], z_next),
-        remote(packed.at[2, 1], passing.at[1], o_send.at[1], o_recv.at[1], z_last),
-        remote(packed.at[3], arrived.at[0], o_send.at[2], o_recv.at[2], z_next),
-        remote(packed.at[1], arrived.at[1], o_send.at[3], o_recv.at[3], z_last),
-        remote(passing.at[0], arrived.at[2, 0], o_send.at[4], o_recv.at[4], z_next),
-        remote(passing.at[1], arrived.at[2, 1], o_send.at[5], o_recv.at[5], z_last),
-    ]
     for step in range(4):
         kv[step].start()
         qs[step].start()
     for step in range(4):
         ws[step].start()
     ws[6].start()
+    announce(0, (z_next, z_last))
 
     ones = jnp.ones((BLK, HEAD), BF16)
     tokens = NB * BLK
@@ -209,20 +203,39 @@
     small_row = lax.broadcasted_iota(jnp.int32, (16, BLK), 0)
 
     def pack(slot, states):
-        tiles = []
         for block, (peak, total, mixed) in enumerate(states):
-            packed[slot, block // HALF, pl.ds(block % HALF * BLK, BLK), :] = (mixed / total).astype(BF16)
+            scaled = (mixed / total).astype(BF16)
             level = peak * EXPONENT + jnp.log(total) * LOG2E
             level = jnp.sum(jnp.where(row == lane, level, 0.0), axis=0, keepdims=True)
             first = level.astype(BF16).astype(F32)
             second = (level - first).astype(BF16).astype(F32)
-            tiles.append((first, second, level - first - second))
-        for half in range(HALF):
-            tile = jnp.zeros((16, BLK), F32)
-            for index in range(HALF):
-                for term in range(3):
-                    tile = jnp.where(small_row == term * HALF + index, tiles[half * HALF + index][term], tile)
-            packed[slot, half, pl.ds(HALF * BLK, 16), :] = tile.astype(BF16)
+            tile = jnp.where(
+                small_row == 0, first,
+                jnp.where(small_row == 1, second, jnp.where(small_row == 2, level - first - second, 0.0)),
+            ).astype(BF16)
+            for half in range(2):
+                packed[slot, 2 * block + half, 0:ROWS, :] = scaled[half * ROWS:(half + 1) * ROWS]
+                packed[slot, 2 * block + half, ROWS:PACKED, :] = tile
+
+    def send(slot):
+        def each(step, carry):
+            receiver = lax.rem(2 * y + RING + step, HEADS)
+            source, target = packed.at[slot, receiver], arrived.at[head, z]
+            here = (slot == 0) & (receiver == head)
+
+            @pl.when(here)
+            def _():
+                pltpu.make_async_copy(source, target, local_sem.at[4]).start()
+
+            @pl.when(jnp.logical_not(here))
+            def _():
+                remote(
+                    source, target, o_send.at[slot], o_recv.at[head], at(x, turn(z, -slot), receiver)
+                ).start()
+
+            return carry
+
+        lax.fori_loop(0, HEADS, each, 0)
 
     every = range(NB)
     qs[0].wait_recv()
@@ -231,6 +244,8 @@
     qs[5].start()
     for copy in own[:3]:
         copy.wait()
+    pl.semaphore_wait(ready.at[0], 2)
+    announce(1, (y_next, y_last))
 
     def own_keys(step, carry):
         slot = step + lax.div(step, 2) - 2 * lax.div(step, 3)
@@ -243,6 +258,8 @@
             kv[5].start()
             qs[2].wait_recv()
             qs[3].wait_recv()
+            pl.semaphore_wait(ready.at[1], 2)
+            announce(2, (y_next, y_last))
 
         @pl.when(step == 3)
         def _():
@@ -252,6 +269,8 @@
             ws[5].start()
             qs[4].wait_recv()
             qs[5].wait_recv()
+            pl.semaphore_wait(ready.at[2], 2)
+            announce(3, (pair,))
 
         ahead = turn(z, -slot) - z
         distance = jnp.maximum(ahead, -ahead)
@@ -300,16 +319,17 @@
 
     lax.fori_loop(0, RING, near_keys, 0)
 
+    pl.semaphore_wait(ready.at[3], 1)
     far_frame = turn(x, 2) * RING + z
 
     def closing(step, carry):
-        late, place = lax.div(step, RING - 1), lax.rem(step, RING - 1)
-        slot = lax.rem(2 + place + lax.div(place, 2), RING)
+        late, place = lax.div(step, RING), lax.rem(step, RING)
+        slot = lax.rem(2 + 3 * place + 3 * lax.div(place, 2) + 2 * lax.div(place, 3), RING)
         this = query_frame(slot)
         distance = jnp.maximum(this - far_frame, far_frame - this)
         needs = distance <= RADIUS
 
-        @pl.when(step == RING - 1)
+        @pl.when(step == RING)
         def _():
             kv[4].wait_recv()
             kv[5].wait_recv()
@@ -322,69 +342,41 @@
         def _():
             pack(slot, attend(slot, [narrow(slot, distance, k_2, v_2, None, 1)], False, every))
 
-        done = needs == (late == 1)
-
-        @pl.when(done & (slot == 2))
-        def _():
-            os[0].start()
-            os[1].start()
-
-        @pl.when(done & (slot == 3))
-        def _():
-            os[2].start()
-
-        @pl.when(done & (slot == 1))
-        def _():
-            os[3].start()
+        @pl.when(needs == (late == 1))
+        def _():
+            send(slot)
 
         return carry
 
-    lax.fori_loop(0, 2 * (RING - 1), closing, 0)
-    os[0].wait_recv()
-    os[4].start()
-    os[1].wait_recv()
-    os[5].start()
+    lax.fori_loop(0, 2 * RING, closing, 0)
     ws[2].wait_recv()
     ws[7].start()
     ws[3].wait_recv()
     ws[8].start()
-    for step in range(2, 6):
-        os[step].wait_recv()
-
-    for block in every:
-        half, place = block // HALF, block % HALF
-        peak, total, mixed = peak_ref[0, block] * EXPONENT, total_ref[0, block], mixed_ref[0, block]
-        levels = []
-        for part in range(RING - 1):
-            tile = arrived[part, half, pl.ds(HALF * BLK, 16), :].astype(F32)
-            level = jnp.sum(jnp.where(lax.rem(small_row, HALF) == place, tile, 0.0), axis=0, keepdims=True)
-            level = jnp.where(row == lane, jnp.broadcast_to(level, (BLK, BLK)), 0.0)
-            levels.append(jnp.sum(level, axis=1, keepdims=True))
-        top_level = jnp.maximum(functools.reduce(jnp.maximum, levels), peak)
-        share = jnp.exp2(peak - top_level)
-        total, mixed = total * share, mixed * share
-        for part in range(RING - 1):
-            share = jnp.exp2(levels[part] - top_level)
-            total += share
-            mixed += arrived[part, half, pl.ds(place * BLK, BLK), :].astype(F32) * share
-        merged = (mixed / total).astype(BF16)
-        rows_out[2 * block] = merged[:ROWS]
-        rows_out[2 * block + 1] = merged[ROWS:]
-
-    mine = pltpu.make_async_copy(rows_out.at[head], rows_in.at[head], local_sem.at[4])
-    to_heads = [
-        remote(rows_out.at[other], rows_in.at[head], a_send.at[index], a_recv.at[head], at(x, z, other))
-        for index, other in enumerate(others)
-    ]
-    for copy in to_heads:
-        copy.start()
-    mine.start()
-
     ws[4].wait_recv()
     ws[5].wait_recv()
     ws[9].start()
+
+    column = lax.broadcasted_iota(jnp.int32, (ROWS, HEAD), 1)
+    here = lax.broadcasted_iota(jnp.int32, (ROWS, HEAD), 0) + core * ROWS
+
+    def merge(other):
+        levels = []
+        for part in range(RING):
+            tile = arrived[other, part, ROWS:PACKED, :].astype(F32)
+            levels.append(jnp.sum(tile, axis=0, keepdims=True))
+        peak = functools.reduce(jnp.maximum, levels)
+        shares = [jnp.exp2(level - peak) for level in levels]
+        whole = functools.reduce(jnp.add, shares)
+        merged = jnp.zeros((ROWS, HEAD), F32)
+        for part in range(RING):
+            share = jnp.broadcast_to(shares[part] / whole, (ROWS, HEAD))
+            share = jnp.sum(jnp.where(column == here, share, 0.0), axis=1, keepdims=True)
+            merged += arrived[other, part, 0:ROWS, :].astype(F32) * share
+        return merged.astype(BF16)
+
+    pltpu.make_async_copy(packed.at[0, head], arrived.at[head, z], local_sem.at[4]).wait()
     own[3].wait()
-    mine.wait()
     for step in range(6, 9):
         ws[step].wait_recv()
 
@@ -396,11 +388,16 @@
         for side in range(2):
             other = chip * 2 + side
 
+            @pl.when(other == head)
+            def _():
+                three = arrived.at[other, pl.ds(0, RING - 1)]
+                pltpu.make_async_copy(three, three, o_recv.at[other]).wait()
+
             @pl.when(other != head)
             def _():
-                pltpu.make_async_copy(rows_in.at[other], rows_in.at[other], a_recv.at[other]).wait()
-
-        left = jnp.concatenate([rows_in[chip * 2], rows_in[chip * 2 + 1]], axis=1)
+                pltpu.make_async_copy(arrived.at[other], arrived.at[other], o_recv.at[other]).wait()
+
+        left = jnp.concatenate([merge(chip * 2), merge(chip * 2 + 1)], axis=1)
         for start in range(0, columns, tile):
             weight = w_all[pl.ds(chip * 2, 2), :, start:start + tile].reshape(2 * HEAD, tile)
             term = jnp.dot(left, weight, preferred_element_type=F32)
@@ -409,10 +406,14 @@
             if index < RING - 1:
                 sums[:, start:start + tile] = term
             else:
-                out_ref[:, start:start + tile] = term.astype(BF16)
-
-    for copy in kv + qs + ws + os + to_heads:
+                out_ref[:, start:start + tile] = term
+
+    for copy in kv + qs + ws:
         copy.wait_send()
+    seven = packed.at[0, pl.ds(0, HEADS - 1)]
+    pltpu.make_async_copy(seven, seven, o_send.at[0]).wait()
+    for slot in range(1, RING):
+        pltpu.make_async_copy(packed.at[slot], packed.at[slot], o_send.at[slot]).wait()
 
 
 def on_device(queries, keys, values, band_width, band_offset, out_weight):
@@ -425,7 +426,7 @@
     smem, anywhere = pl.BlockSpec(memory_space=pltpu.SMEM), pl.BlockSpec(memory_space=pltpu.HBM)
     return pl.pallas_call(
         kernel,
-        out_shape=jax.ShapeDtypeStruct((ROWS, width), BF16),
+        out_shape=jax.ShapeDtypeStruct((ROWS, width), F32),
         in_specs=[smem, smem] + [anywhere] * 4,
         out_specs=pl.BlockSpec(memory_space=pltpu.VMEM),
         scratch_shapes=[block] * 8
@@ -433,19 +434,16 @@
             pltpu.VMEM((RING, NB, BLK, HEAD), BF16),
             pltpu.VMEM((HEADS, HEAD, width), BF16),
             state, state, state,
-            pltpu.VMEM((RING, 2, PACKED, HEAD), BF16),
-            pltpu.VMEM((2, PACKED, HEAD), BF16),
-            pltpu.VMEM((RING - 1, 2, PACKED, HEAD), BF16),
-            pltpu.VMEM((HEADS, ROWS, HEAD), BF16),
-            pltpu.VMEM((HEADS, ROWS, HEAD), BF16),
+            pltpu.VMEM((RING, HEADS, PACKED, HEAD), BF16),
+            pltpu.VMEM((HEADS, RING, PACKED, HEAD), BF16),
             pltpu.VMEM((ROWS, width), F32),
             dma((5,)), dma((6,)), dma((6,)), dma((6,)), dma((6,)), dma((10,)), dma((10,)),
-            dma((6,)), dma((6,)), dma((HEADS - 1,)), dma((HEADS,)),
+            dma((RING,)), dma((HEADS,)), pltpu.SemaphoreType.REGULAR((4,)),
         ],
         compiler_params=pltpu.CompilerParams(
             collective_id=0, has_side_effects=True, vmem_limit_bytes=64 * 1024 * 1024
         ),
-    )(band_width, band_offset, queries, keys, values, out_weight)
+    )(band_width, band_offset, queries, keys, values, out_weight).astype(BF16)
 
 
 def solution(mesh):

time: 36 us -> 34.7 us (0.964)
  other arithmetic: 0 us -> 1.69 us
  local copies, waits for them, and re-layouts: 1.62 us -> 0 us
  Pallas kernels: 34.1 us -> 32.8 us
    convert_element_type x0 -> x1, other arithmetic: none -> 1.69 us  [on_device(): return pl.pallas_call(kernel, out_shape=jax.ShapeDtypeStruct((ROWS, width...]
    unnamed x1 -> x0, local copies, waits for them, and re-layouts: 1.62 us -> none
    pallas_call x1, Pallas kernels: 34.1 us -> 32.8 us  [on_device(): pl.pallas_call(kernel, out_shape=jax.ShapeDtypeStruct((ROWS, width), F32)...]
where the time goes in v3:
time: 34.7 us; the launch traced here: 34.5 us
  Pallas kernels  32.8 us (95%)
  other arithmetic  1.69 us (5%)
    pallas_call x1, Pallas kernels, on_device(): pl.pallas_call(kernel, out_shape=jax.ShapeDtypeStruct((ROWS, width), F32)...  32.8 us
    convert_element_type x1, other arithmetic, on_device(): return pl.pallas_call(kernel, out_shape=jax.ShapeDtypeStruct((ROWS, width...  1.69 us

profile of v3, /device:TPU:1, one launch (start us, length us, event | category | flops | bytes accessed | tf_op | source)
XLA Modules:
  0.0 34.5 jit_solution(13260097299099478323)
XLA Ops:
  0.0 32.8 %shard_map.64 = f32[64,1536]{1,0:T(8,128)} custom-call(s32[8,16]{1,0:T(8,128)} %bitcast.9, s32[8,4,16]{2,1,0:T(4,128)} %bitcast.8, bf16[4,128,128]{2,1,0:T(8,128)(2,1)} %bitcast.5, bf16[4,128,128]{2,1,0:T(8,128)(2,1)} %bitcast.6, bf16[4,128,128]{2,1,0:T(8,128)(2,1)} %bitcast.7, bf16[128,1536]{1,0:T(8,128)(2,1)} %w_hbm.1), custom_call_target="tpu_custom_call" | custom-call | tf_op jit(solution)/shard_map/pallas_call | solution.py:427
  32.8 1.7 %convert_element_type.3 = bf16[64,1536]{1,0:T(8,128)(2,1)} convert(f32[64,1536]{1,0:T(8,128)} %shard_map.64) | non-fusion elementwise | flops 98304 | bytes 589824 | tf_op jit(solution)/shard_map/convert_element_type | solution.py:446

commit v4 on v3

--- a/solution.py
+++ b/solution.py
@@ -88,25 +88,46 @@
         remote(q_all.at[1, low], q_all.at[2, low], q_send.at[4], q_recv.at[4], z_next),
         remote(q_all.at[3, high], q_all.at[2, high], q_send.at[5], q_recv.at[5], z_last),
     ]
-    top, end = pl.ds(0, HEAD // 2), pl.ds(HEAD // 2, HEAD // 2)
-    ws = [
-        remote(w_hbm.at[top], w_all.at[head, top], w_send.at[0], w_recv.at[0], y_next),
-        remote(w_hbm.at[end], w_all.at[head, end], w_send.at[1], w_recv.at[1], y_last),
-        remote(w_hbm.at[end], w_all.at[head, end], w_send.at[2], w_recv.at[2], y_next),
-        remote(w_hbm.at[top], w_all.at[head, top], w_send.at[3], w_recv.at[3], y_last),
-        remote(w_all.at[head_last, top], w_all.at[head_last, top], w_send.at[4], w_recv.at[4], y_next),
-        remote(w_all.at[head_next, end], w_all.at[head_next, end], w_send.at[5], w_recv.at[5], y_last),
-        remote(w_hbm, w_all.at[head], w_send.at[6], w_recv.at[6], pair),
-        remote(w_all.at[head_last], w_all.at[head_last], w_send.at[7], w_recv.at[7], pair),
-        remote(w_all.at[head_next], w_all.at[head_next], w_send.at[8], w_recv.at[8], pair),
-        remote(w_all.at[head_far], w_all.at[head_far], w_send.at[9], w_recv.at[9], pair),
+    part_rows = HEAD // RING
+
+    def quarter(which, begin=0, size=part_rows):
+        return pl.ds(pl.multiple_of(which * part_rows + begin, part_rows // 2), size)
+
+    def weights(source, shard, rows, sem, device, send=None):
+        return remote(
+            source, w_all.at[shard, rows], w_send.at[sem if send is None else send], w_recv.at[sem], device
+        )
+
+    half_rows, later = part_rows // 2, HEAD - part_rows
+    direct = [
+        weights(w_hbm.at[quarter(turn(x, step))], head, quarter(turn(x, step)), side + min(step, 1), device)
+        for step in range(RING) for side, device in ((0, y_next), (2, y_last))
     ]
+
+    def passed(shard, which, begin, size, sem, device):
+        rows = quarter(which, begin, size)
+        return weights(w_all.at[shard, rows], shard, rows, sem, device)
+
+    every_row = pl.ds(0, HEAD)
+    ws = {
+        4: passed(head_last, x, 0, half_rows, 4, y_next),
+        5: passed(head_next, x, half_rows, half_rows, 5, y_last),
+        6: passed(head_far, x, 0, part_rows, 6, x_next),
+        7: passed(head_far, x, 0, part_rows, 7, x_last),
+        8: passed(head_far, turn(x, -1), 0, half_rows, 8, x_next),
+        9: passed(head_far, turn(x, 1), half_rows, half_rows, 9, x_last),
+        10: weights(w_hbm, head, every_row, 10, pair),
+        11: weights(w_all.at[head_last], head_last, every_row, 11, pair),
+        12: weights(w_all.at[head_next], head_next, every_row, 12, pair),
+        13: weights(w_all.at[head_far], head_far, every_row, 13, pair),
+    }
+    several = w_all.at[head, pl.ds(0, later)]
     for step in range(4):
         kv[step].start()
         qs[step].start()
-    for step in range(4):
-        ws[step].start()
-    ws[6].start()
+    for copy in direct[:6]:
+        copy.start()
+    ws[10].start()
     announce(0, (z_next, z_last))
 
     ones = jnp.ones((BLK, HEAD), BF16)
@@ -258,15 +279,17 @@
             kv[5].start()
             qs[2].wait_recv()
             qs[3].wait_recv()
+            direct[0].wait_recv()
+            ws[4].start()
+            direct[1].wait_recv()
+            ws[5].start()
+            for copy in direct[6:]:
+                copy.start()
             pl.semaphore_wait(ready.at[1], 2)
             announce(2, (y_next, y_last))
 
         @pl.when(step == 3)
         def _():
-            ws[0].wait_recv()
-            ws[4].start()
-            ws[1].wait_recv()
-            ws[5].start()
             qs[4].wait_recv()
             qs[5].wait_recv()
             pl.semaphore_wait(ready.at[2], 2)
@@ -319,43 +342,41 @@
 
     lax.fori_loop(0, RING, near_keys, 0)
 
+    ws[4].wait_recv()
+    ws[5].wait_recv()
+    ws[6].start()
+    ws[7].start()
     pl.semaphore_wait(ready.at[3], 1)
     far_frame = turn(x, 2) * RING + z
 
-    def closing(step, carry):
-        late, place = lax.div(step, RING), lax.rem(step, RING)
-        slot = lax.rem(2 + 3 * place + 3 * lax.div(place, 2) + 2 * lax.div(place, 3), RING)
+    def far_keys(slot):
         this = query_frame(slot)
         distance = jnp.maximum(this - far_frame, far_frame - this)
-        needs = distance <= RADIUS
-
-        @pl.when(step == RING)
-        def _():
-            kv[4].wait_recv()
-            kv[5].wait_recv()
-
-        @pl.when((late == 0) & jnp.logical_not(needs))
-        def _():
-            pack(slot, [(peak_ref[slot, b], total_ref[slot, b], mixed_ref[slot, b]) for b in every])
-
-        @pl.when((late == 1) & needs)
-        def _():
-            pack(slot, attend(slot, [narrow(slot, distance, k_2, v_2, None, 1)], False, every))
-
-        @pl.when(needs == (late == 1))
-        def _():
-            send(slot)
-
-        return carry
-
-    lax.fori_loop(0, 2 * RING, closing, 0)
-    ws[2].wait_recv()
-    ws[7].start()
-    ws[3].wait_recv()
+        source = narrow(slot, jnp.minimum(distance, RADIUS), k_2, v_2, distance <= RADIUS, 1)
+        return attend(slot, [source], False, every)
+
+    pack(0, [(peak_ref[0, b], total_ref[0, b], mixed_ref[0, b]) for b in every])
+    send(0)
+    kv[4].wait_recv()
+    kv[5].wait_recv()
+    pack(2, far_keys(2))
+    send(2)
+    states = far_keys(3), far_keys(1)
+    pack(3, states[0])
+    pack(1, states[1])
+    send(3)
+    send(1)
+    ws[6].wait_recv()
     ws[8].start()
-    ws[4].wait_recv()
-    ws[5].wait_recv()
+    ws[7].wait_recv()
     ws[9].start()
+    pltpu.make_async_copy(several, several, w_recv.at[1]).wait()
+    ws[11].start()
+    pltpu.make_async_copy(several, several, w_recv.at[3]).wait()
+    ws[12].start()
+    ws[8].wait_recv()
+    ws[9].wait_recv()
+    ws[13].start()
 
     column = lax.broadcasted_iota(jnp.int32, (ROWS, HEAD), 1)
     here = lax.broadcasted_iota(jnp.int32, (ROWS, HEAD), 0) + core * ROWS
@@ -377,14 +398,14 @@
 
     pltpu.make_async_copy(packed.at[0, head], arrived.at[head, z], local_sem.at[4]).wait()
     own[3].wait()
-    for step in range(6, 9):
+    for step in range(10, 13):
         ws[step].wait_recv()
 
     columns, tile = w_all.shape[2], 512
     for index, step in enumerate((0, -1, 1, 2)):
         chip = turn(y, step)
         if step == 2:
-            ws[9].wait_recv()
+            ws[13].wait_recv()
         for side in range(2):
             other = chip * 2 + side
 
@@ -408,8 +429,10 @@
             else:
                 out_ref[:, start:start + tile] = term
 
-    for copy in kv + qs + ws:
+    for copy in kv + qs + direct[:2] + list(ws.values()):
         copy.wait_send()
+    for sem in (1, 3):
+        pltpu.make_async_copy(several, several, w_send.at[sem]).wait()
     seven = packed.at[0, pl.ds(0, HEADS - 1)]
     pltpu.make_async_copy(seven, seven, o_send.at[0]).wait()
     for slot in range(1, RING):
@@ -420,6 +443,10 @@
     width = out_weight.shape[1]
     queries, keys, values = (array.reshape(NB, BLK, HEAD) for array in (queries, keys, values))
     band_width, band_offset = band_width.T, band_offset.transpose(1, 2, 0)
+    band_width, band_offset, queries, keys, values, out_weight = (
+        pltpu.with_memory_space_constraint(array, pltpu.HBM)
+        for array in (band_width, band_offset, queries, keys, values, out_weight)
+    )
     block = pltpu.VMEM((NB, BLK, HEAD), BF16)
     state = pltpu.VMEM((RING, NB, BLK, HEAD), F32)
     dma = pltpu.SemaphoreType.DMA
@@ -437,11 +464,11 @@
             pltpu.VMEM((RING, HEADS, PACKED, HEAD), BF16),
             pltpu.VMEM((HEADS, RING, PACKED, HEAD), BF16),
             pltpu.VMEM((ROWS, width), F32),
-            dma((5,)), dma((6,)), dma((6,)), dma((6,)), dma((6,)), dma((10,)), dma((10,)),
+            dma((5,)), dma((6,)), dma((6,)), dma((6,)), dma((6,)), dma((14,)), dma((14,)),
             dma((RING,)), dma((HEADS,)), pltpu.SemaphoreType.REGULAR((4,)),
         ],
         compiler_params=pltpu.CompilerParams(
-            collective_id=0, has_side_effects=True, vmem_limit_bytes=64 * 1024 * 1024
+            collective_id=0, has_side_effects=True, vmem_limit_bytes=52 * 1024 * 1024
         ),
     )(band_width, band_offset, queries, keys, values, out_weight).astype(BF16)
 

time: 34.7 us -> 31.2 us (0.90)
  Pallas kernels: 32.8 us -> 30.3 us
  other arithmetic: 1.69 us -> 0.7 us
    pallas_call x1, Pallas kernels: 32.8 us -> 30.3 us  [on_device(): pl.pallas_call(kernel, out_shape=jax.ShapeDtypeStruct((ROWS, width), F32)...]
    convert_element_type x1, other arithmetic: 1.69 us -> 0.7 us  [on_device(): return pl.pallas_call(kernel, out_shape=jax.ShapeDtypeStruct((ROWS, width...]
where the time goes in v4:
time: 31.2 us; the launch traced here: 31 us
  Pallas kernels  30.3 us (97%)
  other arithmetic  0.7 us (2%)
    pallas_call x1, Pallas kernels, on_device(): pl.pallas_call(kernel, out_shape=jax.ShapeDtypeStruct((ROWS, width), F32)...  30.3 us
    convert_element_type x1, other arithmetic, on_device(): return pl.pallas_call(kernel, out_shape=jax.ShapeDtypeStruct((ROWS, width...  0.7 us

profile of v4, /device:TPU:1, one launch (start us, length us, event | category | flops | bytes accessed | tf_op | source)
XLA Modules:
  0.0 31.0 jit_solution(9596117056784337263)
XLA Ops:
  0.0 30.3 %shard_map.64 = f32[64,1536]{1,0:T(8,128)S(1)} custom-call(s32[8,16]{1,0:T(8,128)} %bitcast.9, s32[8,4,16]{2,1,0:T(4,128)} %bitcast.8, bf16[4,128,128]{2,1,0:T(8,128)(2,1)} %bitcast.5, bf16[4,128,128]{2,1,0:T(8,128)(2,1)} %bitcast.6, bf16[4,128,128]{2,1,0:T(8,128)(2,1)} %bitcast.7, bf16[128,1536]{1,0:T(8,128)(2,1)} %w_hbm.1), custom_call_target="tpu_custom_call" | custom-call | tf_op jit(solution)/shard_map/pallas_call | solution.py:454
  30.3 0.7 %convert_element_type.3 = bf16[64,1536]{1,0:T(8,128)(2,1)} convert(f32[64,1536]{1,0:T(8,128)S(1)} %shard_map.64) | non-fusion elementwise | flops 98304 | bytes 589824 | tf_op jit(solution)/shard_map/convert_element_type | solution.py:473

commit v5 on v4

--- a/solution.py
+++ b/solution.py
@@ -16,7 +16,7 @@
 RADIUS = 7
 ROWS = 64
 HALF = NB // 2
-PACKED = ROWS + 16
+PACKED = ROWS + 8
 LOG2E = math.log2(math.e)
 EXPONENT = LOG2E / math.sqrt(HEAD)
 LOW = -1e30
@@ -221,7 +221,7 @@
 
     row = lax.broadcasted_iota(jnp.int32, (BLK, BLK), 0)
     lane = lax.broadcasted_iota(jnp.int32, (BLK, BLK), 1)
-    small_row = lax.broadcasted_iota(jnp.int32, (16, BLK), 0)
+    small_row = lax.broadcasted_iota(jnp.int32, (8, BLK), 0)
 
     def pack(slot, states):
         for block, (peak, total, mixed) in enumerate(states):

time: 31.2 us -> 30.7 us (0.984)
  Pallas kernels: 30.3 us -> 29.7 us
    pallas_call x1, Pallas kernels: 30.3 us -> 29.7 us  [on_device(): pl.pallas_call(kernel, out_shape=jax.ShapeDtypeStruct((ROWS, width), F32)...]
where the time goes in v5:
time: 30.7 us; the launch traced here: 30.4 us
  Pallas kernels  29.7 us (97%)
  other arithmetic  0.7 us (2%)
    pallas_call x1, Pallas kernels, on_device(): pl.pallas_call(kernel, out_shape=jax.ShapeDtypeStruct((ROWS, width), F32)...  29.7 us
    convert_element_type x1, other arithmetic, on_device(): return pl.pallas_call(kernel, out_shape=jax.ShapeDtypeStruct((ROWS, width...  0.7 us

profile of v5, /device:TPU:1, one launch (start us, length us, event | category | flops | bytes accessed | tf_op | source)
XLA Modules:
  0.0 30.4 jit_solution(1879627082462556703)
XLA Ops:
  0.0 29.7 %shard_map.64 = f32[64,1536]{1,0:T(8,128)S(1)} custom-call(s32[8,16]{1,0:T(8,128)} %bitcast.9, s32[8,4,16]{2,1,0:T(4,128)} %bitcast.8, bf16[4,128,128]{2,1,0:T(8,128)(2,1)} %bitcast.5, bf16[4,128,128]{2,1,0:T(8,128)(2,1)} %bitcast.6, bf16[4,128,128]{2,1,0:T(8,128)(2,1)} %bitcast.7, bf16[128,1536]{1,0:T(8,128)(2,1)} %w_hbm.1), custom_call_target="tpu_custom_call" | custom-call | tf_op jit(solution)/shard_map/pallas_call | solution.py:454
  29.7 0.7 %convert_element_type.3 = bf16[64,1536]{1,0:T(8,128)(2,1)} convert(f32[64,1536]{1,0:T(8,128)S(1)} %shard_map.64) | non-fusion elementwise | flops 98304 | bytes 589824 | tf_op jit(solution)/shard_map/convert_element_type | solution.py:473

commit v6 on v5

--- a/solution.py
+++ b/solution.py
@@ -29,8 +29,8 @@
 
 
 def kernel(
-    width_ref, offset_ref, q_hbm, k_hbm, v_hbm, w_hbm, out_ref,
-    k_0, k_1, k_2, k_3, v_0, v_1, v_2, v_3, q_all, w_all,
+    width_hbm, offset_hbm, q_hbm, k_hbm, v_hbm, w_hbm, out_ref,
+    width_ref, offset_ref, k_0, k_1, k_2, k_3, v_0, v_1, v_2, v_3, q_all, w_all,
     peak_ref, total_ref, mixed_ref, packed, arrived, sums,
     local_sem, kv_send, kv_recv, q_send, q_recv, w_send, w_recv, o_send, o_recv, ready,
 ):
@@ -66,6 +66,8 @@
         pltpu.make_async_copy(k_hbm, k_0, local_sem.at[1]),
         pltpu.make_async_copy(v_hbm, v_0, local_sem.at[2]),
         pltpu.make_async_copy(w_hbm, w_all.at[head], local_sem.at[3]),
+        pltpu.make_async_copy(width_hbm, width_ref, local_sem.at[5]),
+        pltpu.make_async_copy(offset_hbm, offset_ref, local_sem.at[6]),
     ]
     for copy in own:
         copy.start()
@@ -263,7 +265,7 @@
     qs[4].start()
     qs[1].wait_recv()
     qs[5].start()
-    for copy in own[:3]:
+    for copy in own[:3] + own[4:]:
         copy.wait()
     pl.semaphore_wait(ready.at[0], 2)
     announce(1, (y_next, y_last))
@@ -450,13 +452,14 @@
     block = pltpu.VMEM((NB, BLK, HEAD), BF16)
     state = pltpu.VMEM((RING, NB, BLK, HEAD), F32)
     dma = pltpu.SemaphoreType.DMA
-    smem, anywhere = pl.BlockSpec(memory_space=pltpu.SMEM), pl.BlockSpec(memory_space=pltpu.HBM)
+    anywhere = pl.BlockSpec(memory_space=pltpu.HBM)
     return pl.pallas_call(
         kernel,
         out_shape=jax.ShapeDtypeStruct((ROWS, width), F32),
-        in_specs=[smem, smem] + [anywhere] * 4,
+        in_specs=[anywhere] * 6,
         out_specs=pl.BlockSpec(memory_space=pltpu.VMEM),
-        scratch_shapes=[block] * 8
+        scratch_shapes=[pltpu.SMEM(band_width.shape, jnp.int32), pltpu.SMEM(band_offset.shape, jnp.int32)]
+        + [block] * 8
         + [
             pltpu.VMEM((RING, NB, BLK, HEAD), BF16),
             pltpu.VMEM((HEADS, HEAD, width), BF16),
@@ -464,7 +467,7 @@
             pltpu.VMEM((RING, HEADS, PACKED, HEAD), BF16),
             pltpu.VMEM((HEADS, RING, PACKED, HEAD), BF16),
             pltpu.VMEM((ROWS, width), F32),
-            dma((5,)), dma((6,)), dma((6,)), dma((6,)), dma((6,)), dma((14,)), dma((14,)),
+            dma((7,)), dma((6,)), dma((6,)), dma((6,)), dma((6,)), dma((14,)), dma((14,)),
             dma((RING,)), dma((HEADS,)), pltpu.SemaphoreType.REGULAR((4,)),
         ],
         compiler_params=pltpu.CompilerParams(

time: 30.7 us -> 29.6 us (0.964)
  Pallas kernels: 29.7 us -> 28.7 us
    pallas_call x1, Pallas kernels: 29.7 us -> 28.7 us  [on_device(): pl.pallas_call(kernel, out_shape=jax.ShapeDtypeStruct((ROWS, width), F32)...]
where the time goes in v6:
time: 29.6 us; the launch traced here: 29.5 us
  Pallas kernels  28.7 us (97%)
  other arithmetic  0.7 us (2%)
    pallas_call x1, Pallas kernels, on_device(): pl.pallas_call(kernel, out_shape=jax.ShapeDtypeStruct((ROWS, width), F32)...  28.7 us
    convert_element_type x1, other arithmetic, on_device(): return pl.pallas_call(kernel, out_shape=jax.ShapeDtypeStruct((ROWS, width...  0.7 us

profile of v6, /device:TPU:1, one launch (start us, length us, event | category | flops | bytes accessed | tf_op | source)
XLA Modules:
  0.0 29.5 jit_solution(4678222163688687669)
XLA Ops:
  0.0 28.7 %shard_map.64 = f32[64,1536]{1,0:T(8,128)S(1)} custom-call(s32[8,16]{1,0:T(8,128)} %bitcast.9, s32[8,4,16]{2,1,0:T(4,128)} %bitcast.8, bf16[4,128,128]{2,1,0:T(8,128)(2,1)} %bitcast.5, bf16[4,128,128]{2,1,0:T(8,128)(2,1)} %bitcast.6, bf16[4,128,128]{2,1,0:T(8,128)(2,1)} %bitcast.7, bf16[128,1536]{1,0:T(8,128)(2,1)} %w_hbm.1), custom_call_target="tpu_custom_call" | custom-call | tf_op jit(solution)/shard_map/pallas_call | solution.py:456
  28.8 0.7 %convert_element_type.3 = bf16[64,1536]{1,0:T(8,128)(2,1)} convert(f32[64,1536]{1,0:T(8,128)S(1)} %shard_map.64) | non-fusion elementwise | flops 98304 | bytes 589824 | tf_op jit(solution)/shard_map/convert_element_type | solution.py:476

commit v7 on v6

--- a/solution.py
+++ b/solution.py
@@ -228,8 +228,10 @@
     def pack(slot, states):
         for block, (peak, total, mixed) in enumerate(states):
             scaled = (mixed / total).astype(BF16)
+            peak, total = (
+                jnp.sum(jnp.where(row == lane, term, 0.0), axis=0, keepdims=True) for term in (peak, total)
+            )
             level = peak * EXPONENT + jnp.log(total) * LOG2E
-            level = jnp.sum(jnp.where(row == lane, level, 0.0), axis=0, keepdims=True)
             first = level.astype(BF16).astype(F32)
             second = (level - first).astype(BF16).astype(F32)
             tile = jnp.where(
@@ -363,10 +365,9 @@
     kv[5].wait_recv()
     pack(2, far_keys(2))
     send(2)
-    states = far_keys(3), far_keys(1)
-    pack(3, states[0])
-    pack(1, states[1])
+    pack(3, far_keys(3))
     send(3)
+    pack(1, far_keys(1))
     send(1)
     ws[6].wait_recv()
     ws[8].start()

time: 29.6 us -> 29.5 us (level)
  no operation moved by 1% of the time
where the time goes in v7:
time: 29.5 us; the launch traced here: 29.4 us
  Pallas kernels  28.7 us (97%)
  other arithmetic  0.7 us (2%)
    pallas_call x1, Pallas kernels, on_device(): pl.pallas_call(kernel, out_shape=jax.ShapeDtypeStruct((ROWS, width), F32)...  28.7 us
    convert_element_type x1, other arithmetic, on_device(): return pl.pallas_call(kernel, out_shape=jax.ShapeDtypeStruct((ROWS, width...  0.7 us

profile of v7, /device:TPU:1, one launch (start us, length us, event | category | flops | bytes accessed | tf_op | source)
XLA Modules:
  0.0 29.4 jit_solution(2926605148602702099)
XLA Ops:
  0.0 28.7 %shard_map.64 = f32[64,1536]{1,0:T(8,128)S(1)} custom-call(s32[8,16]{1,0:T(8,128)} %bitcast.9, s32[8,4,16]{2,1,0:T(4,128)} %bitcast.8, bf16[4,128,128]{2,1,0:T(8,128)(2,1)} %bitcast.5, bf16[4,128,128]{2,1,0:T(8,128)(2,1)} %bitcast.6, bf16[4,128,128]{2,1,0:T(8,128)(2,1)} %bitcast.7, bf16[128,1536]{1,0:T(8,128)(2,1)} %w_hbm.1), custom_call_target="tpu_custom_call" | custom-call | tf_op jit(solution)/shard_map/pallas_call | solution.py:457
  28.8 0.7 %convert_element_type.3 = bf16[64,1536]{1,0:T(8,128)(2,1)} convert(f32[64,1536]{1,0:T(8,128)S(1)} %shard_map.64) | non-fusion elementwise | flops 98304 | bytes 589824 | tf_op jit(solution)/shard_map/convert_element_type | solution.py:477

commit v8 on v6

--- a/solution.py
+++ b/solution.py
@@ -344,10 +344,6 @@
 
     lax.fori_loop(0, RING, near_keys, 0)
 
-    ws[4].wait_recv()
-    ws[5].wait_recv()
-    ws[6].start()
-    ws[7].start()
     pl.semaphore_wait(ready.at[3], 1)
     far_frame = turn(x, 2) * RING + z
 
@@ -361,6 +357,10 @@
     send(0)
     kv[4].wait_recv()
     kv[5].wait_recv()
+    ws[4].wait_recv()
+    ws[5].wait_recv()
+    ws[6].start()
+    ws[7].start()
     pack(2, far_keys(2))
     send(2)
     states = far_keys(3), far_keys(1)

time: 29.6 us -> 29.9 us (1.010)
  Pallas kernels: 28.7 us -> 29.1 us
    pallas_call x1, Pallas kernels: 28.7 us -> 29.1 us  [on_device(): pl.pallas_call(kernel, out_shape=jax.ShapeDtypeStruct((ROWS, width), F32)...]
where the time goes in v8:
time: 29.9 us; the launch traced here: 29.8 us
  Pallas kernels  29.1 us (97%)
  other arithmetic  0.7 us (2%)
    pallas_call x1, Pallas kernels, on_device(): pl.pallas_call(kernel, out_shape=jax.ShapeDtypeStruct((ROWS, width), F32)...  29.1 us
    convert_element_type x1, other arithmetic, on_device(): return pl.pallas_call(kernel, out_shape=jax.ShapeDtypeStruct((ROWS, width...  0.7 us

profile of v8, /device:TPU:1, one launch (start us, length us, event | category | flops | bytes accessed | tf_op | source)
XLA Modules:
  0.0 29.8 jit_solution(16209396812357360781)
XLA Ops:
  0.0 29.1 %shard_map.64 = f32[64,1536]{1,0:T(8,128)S(1)} custom-call(s32[8,16]{1,0:T(8,128)} %bitcast.9, s32[8,4,16]{2,1,0:T(4,128)} %bitcast.8, bf16[4,128,128]{2,1,0:T(8,128)(2,1)} %bitcast.5, bf16[4,128,128]{2,1,0:T(8,128)(2,1)} %bitcast.6, bf16[4,128,128]{2,1,0:T(8,128)(2,1)} %bitcast.7, bf16[128,1536]{1,0:T(8,128)(2,1)} %w_hbm.1), custom_call_target="tpu_custom_call" | custom-call | tf_op jit(solution)/shard_map/pallas_call | solution.py:456
  29.1 0.7 %convert_element_type.3 = bf16[64,1536]{1,0:T(8,128)(2,1)} convert(f32[64,1536]{1,0:T(8,128)S(1)} %shard_map.64) | non-fusion elementwise | flops 98304 | bytes 589824 | tf_op jit(solution)/shard_map/convert_element_type | solution.py:476
